TPU v7x, 32 devices: a whole 2x2x4 slice. The times are simulated.
32 devices in a mesh: dp: 32 (over z, y, x, core).
Axes of the slice: x: 2, y: 2, z: 4, core: 2. Of those that a mesh axis runs over, the one named last changes fastest.
Arguments:
- tokens: bfloat16 [2, 5120, 1024], P(None, 'dp'), may hold values from -6 to 6
- grad_out: bfloat16 [2, 5120, 1024], P(None, 'dp'), may hold values from -6 to 6
- w_query: bfloat16 [1024, 1024], P('dp'), may hold values from -0.1875 to 0.1875
- w_key: bfloat16 [1024, 1024], P('dp'), may hold values from -0.1875 to 0.1875
- w_value: bfloat16 [1024, 1024], P('dp'), may hold values from -0.1875 to 0.1875
- b_query: bfloat16 [1024], P('dp'), may hold values from -3 to 3
- b_value: bfloat16 [1024], P('dp'), may hold values from -3 to 3
- w_attn_out: bfloat16 [1024, 1024], P('dp'), may hold values from -0.75 to 0.75
- b_attn_out: bfloat16 [1024], P('dp'), may hold values from -3 to 3
- w_up: bfloat16 [1024, 4096], P('dp'), may hold values from -0.1875 to 0.1875
- b_up: bfloat16 [4096], P('dp'), may hold values from -3 to 3
- w_down: bfloat16 [4096, 1024], P('dp'), may hold values from -0.09375 to 0.09375
- b_down: bfloat16 [1024], P('dp'), may hold values from -3 to 3
- ln1_gain: bfloat16 [1024], P('dp'), may hold values from 0.25 to 1.75
- ln1_bias: bfloat16 [1024], P('dp'), may hold values from -2 to 2
- ln2_gain: bfloat16 [1024], P('dp'), may hold values from 0.25 to 1.75
- ln2_bias: bfloat16 [1024], P('dp'), may hold values from -2 to 2
- leaf_parent: int32 [2, 4, 8], replicated, may hold values from 1 to 4, as said below
Outputs:
- output: bfloat16 [2, 5120, 1024], P(None, 'dp')
- grad_input: bfloat16 [2, 5120, 1024], P(None, 'dp')
- grad_w_query: float32 [1024, 1024], P('dp')
- grad_w_key: float32 [1024, 1024], P('dp')
- grad_w_value: float32 [1024, 1024], P('dp')
- grad_w_attn_out: float32 [1024, 1024], P('dp')
- grad_w_up: float32 [1024, 4096], P('dp')
- grad_w_down: float32 [4096, 1024], P('dp')
- grad_b_query: float32 [1024], P('dp')
- grad_b_value: float32 [1024], P('dp')
- grad_b_attn_out: float32 [1024], P('dp')
- grad_b_up: float32 [4096], P('dp')
- grad_b_down: float32 [1024], P('dp')
- grad_ln1_gain: float32 [1024], P('dp')
- grad_ln1_bias: float32 [1024], P('dp')
- grad_ln2_gain: float32 [1024], P('dp')
- grad_ln2_bias: float32 [1024], P('dp')
Inputs may be any that keep to these rules, and one draw needn't show every extreme that they name: leaf_parent[m, t, l] is the branch segment of leaf l of tree t; each of the 4 branches of a tree is the parent of exactly 2 leaves.
All inputs are finite; a program needn't handle non-finite values.
Results may differ from a plain program's by a relative error of at most 0.012.
Values may be sent and summed in bfloat16 or wider, within the bound.
No kernel may reach another device: no remote copies, remote signals or barrier semaphores. Data moves between devices by JAX's collectives and lax.ppermute only.
A program may use at most 320 MiB of HBM per device.

v0:
```python
from functools import partial

import jax
import jax.numpy as jnp
from jax import lax
from jax.sharding import PartitionSpec as P

HEADS = 16
BLK_DEV = 5
TRUNK_BLK = 16
SEG_BLK = 2
BRANCHES = 4
TREE_BLK = 40


eps = 1e-05


def from_behind(value, axis, steps):
    count = lax.axis_size(axis)
    leading, last = (max(0, -steps), min(count, count - steps))
    return lax.ppermute(value, axis, [(source, source + steps) for source in range(leading, last)])


def layer_norm(values, gain, shift):
    center = values - jnp.mean(values, axis=-1, keepdims=True)
    spread = jnp.mean(center * center, axis=-1, keepdims=True)
    return center * lax.rsqrt(spread + eps) * gain + shift


def path_info(first_block, count, block_len, parents):
    blocks = first_block + jnp.arange(count, dtype=jnp.int32)
    tree_ids = blocks // TREE_BLK
    local_block = blocks % TREE_BLK
    after_trunk = local_block - TRUNK_BLK
    leaf_part = after_trunk - BRANCHES * SEG_BLK
    is_trunk = local_block < TRUNK_BLK
    is_branch = jnp.logical_and(local_block >= TRUNK_BLK, leaf_part < 0)
    segment = jnp.where(
        is_trunk,
        0,
        jnp.where(is_branch, 1 + after_trunk // SEG_BLK, 1 + BRANCHES + leaf_part // SEG_BLK),
    )
    offset = jnp.where(
        is_trunk,
        local_block,
        jnp.where(
            is_branch, TRUNK_BLK + after_trunk % SEG_BLK, TRUNK_BLK + SEG_BLK + leaf_part % SEG_BLK
        ),
    )
    tree_hit = (tree_ids[:, None] == jnp.arange(parents.shape[0], dtype=jnp.int32)[None, :]).astype(
        jnp.int32
    )
    tree_rows = jnp.sum(tree_hit[:, :, None] * parents[None, :, :], axis=1)
    leaf_hit = (
        (segment - 1 - BRANCHES)[:, None] == jnp.arange(parents.shape[1], dtype=jnp.int32)[None, :]
    ).astype(jnp.int32)
    parent = jnp.sum(leaf_hit * tree_rows, axis=1)
    within = jnp.arange(block_len, dtype=jnp.int32)
    seg_tok = jnp.repeat(segment, block_len)
    par_tok = jnp.repeat(parent, block_len)
    pos_tok = (offset[:, None] * block_len + within[None, :]).reshape(-1)
    return (seg_tok, par_tok, pos_tok)


def visible(query_info, key_info):
    query_seg, query_par, query_pos = query_info
    key_seg, key_par, key_pos = key_info
    related = (
        (key_seg[None, :] == query_seg[:, None])
        | (key_seg[None, :] == 0)
        | (key_seg[None, :] == query_par[:, None])
    )
    return related & (key_pos[None, :] <= query_pos[:, None])


def alibi_bias(query_pos, key_pos, head_count):
    slopes = jnp.exp2(-8.0 * (jnp.arange(head_count, dtype=jnp.float32) + 1.0) / head_count)
    distance = (query_pos[:, None] - key_pos[None, :]).astype(jnp.float32)
    return -slopes[:, None, None] * distance[None, :, :]


def block_scores(query_h, key_h, query_info, key_info, score_scale):
    raw_scores = (
        jnp.einsum("qhd,khd->hqk", query_h, key_h, preferred_element_type=jnp.float32) * score_scale
    )
    raw_scores = raw_scores + alibi_bias(query_info[2], key_info[2], query_h.shape[1])
    return jnp.where(visible(query_info, key_info)[None], raw_scores, -jnp.inf)


def scored(live, query_h, key_h, query_info, key_info, score_scale):
    shape = (query_h.shape[1], query_h.shape[0], key_h.shape[0])
    return lax.cond(
        live,
        partial(block_scores, query_h, key_h, query_info, key_info, score_scale),
        partial(jnp.full, shape, -jnp.inf, jnp.float32),
    )


def add_context(live, context, scores, log_total, value_h):

    def added():
        weights_b = jnp.exp(scores - log_total[:, :, None]).astype(jnp.bfloat16)
        return context + jnp.einsum(
            "hqk,khd->qhd", weights_b, value_h, preferred_element_type=jnp.float32
        )

    return lax.cond(live, added, lambda: context)


def prob_pair(
    live, query_h, key_h, value_h, grad_ctx_h, query_info, key_info, log_total, score_scale
):
    shape = (query_h.shape[1], query_h.shape[0], key_h.shape[0])

    def prob_computed():
        probs = jnp.exp(
            block_scores(query_h, key_h, query_info, key_info, score_scale) - log_total[:, :, None]
        )
        grad_probs = jnp.einsum(
            "qhd,khd->hqk", grad_ctx_h, value_h, preferred_element_type=jnp.float32
        )
        return (probs, grad_probs)

    empty = jnp.zeros(shape, jnp.float32)
    return lax.cond(live, prob_computed, lambda: (empty, empty))


def block_back(live, probs, grad_probs, delta, query_h, key_h, grad_ctx_h, score_scale):
    row_count, head_count, head_dim = query_h.shape
    key_rows = key_h.shape[0]

    def block_computed():
        grad_scores = (probs * (grad_probs - delta[:, :, None])).astype(jnp.bfloat16)
        grad_query = (
            jnp.einsum("hqk,khd->qhd", grad_scores, key_h, preferred_element_type=jnp.float32)
            * score_scale
        )
        grad_key = (
            jnp.einsum("hqk,qhd->khd", grad_scores, query_h, preferred_element_type=jnp.float32)
            * score_scale
        )
        grad_value = jnp.einsum(
            "hqk,qhd->khd",
            probs.astype(jnp.bfloat16),
            grad_ctx_h,
            preferred_element_type=jnp.float32,
        )
        return (
            grad_query,
            jnp.stack(
                (
                    grad_key.reshape(key_rows, head_count * head_dim),
                    grad_value.reshape(key_rows, head_count * head_dim),
                )
            ),
        )

    empty_query = jnp.zeros((row_count, head_count, head_dim), jnp.float32)
    empty_pair = jnp.zeros((2, key_rows, head_count * head_dim), jnp.float32)
    return lax.cond(live, block_computed, lambda: (empty_query, empty_pair))


def gelu_tanh(values):
    return jax.nn.gelu(values, approximate=True)


def on_device(
    tokens,
    grad_out,
    w_query,
    w_key,
    w_value,
    b_query,
    b_value,
    w_attn_out,
    b_attn_out,
    w_up,
    b_up,
    w_down,
    b_down,
    ln1_gain,
    ln1_bias,
    ln2_gain,
    ln2_bias,
    leaf_parent,
):
    shards = (
        w_query,
        w_key,
        w_value,
        w_attn_out,
        w_up,
        w_down,
        b_query,
        b_value,
        b_attn_out,
        b_up,
        b_down,
        ln1_gain,
        ln1_bias,
        ln2_gain,
        ln2_bias,
    )
    micro_count, row_count, feature_width = tokens.shape
    head_count = HEADS
    head_dim = feature_width // head_count
    score_scale = head_dim ** (-0.5)
    block_len = row_count // BLK_DEV
    tree_dev = TREE_BLK // BLK_DEV
    device_index = lax.axis_index("dp")
    tree_place = device_index * BLK_DEV % TREE_BLK // BLK_DEV
    axis_count = lax.axis_size("dp")
    totals = [
        jnp.zeros((piece.shape[0] * axis_count,) + piece.shape[1:], jnp.float32) for piece in shards
    ]
    outputs = []
    input_grads = []
    for micro_index in range(micro_count):
        gathered = (
            lax.all_gather(w_query, "dp", axis=0, tiled=True),
            lax.all_gather(w_key, "dp", axis=0, tiled=True),
            lax.all_gather(w_value, "dp", axis=0, tiled=True),
            lax.all_gather(w_attn_out, "dp", axis=0, tiled=True),
            lax.all_gather(w_up, "dp", axis=0, tiled=True),
            lax.all_gather(w_down, "dp", axis=0, tiled=True),
            lax.all_gather(b_query, "dp", axis=0, tiled=True),
            lax.all_gather(b_value, "dp", axis=0, tiled=True),
            lax.all_gather(b_attn_out, "dp", axis=0, tiled=True),
            lax.all_gather(b_up, "dp", axis=0, tiled=True),
            lax.all_gather(b_down, "dp", axis=0, tiled=True),
            lax.all_gather(ln1_gain, "dp", axis=0, tiled=True),
            lax.all_gather(ln1_bias, "dp", axis=0, tiled=True),
            lax.all_gather(ln2_gain, "dp", axis=0, tiled=True),
            lax.all_gather(ln2_bias, "dp", axis=0, tiled=True),
        )
        (
            mat_query,
            mat_key,
            mat_value,
            mat_out,
            mat_up,
            mat_down,
            vec_query,
            vec_value,
            vec_out,
            vec_up,
            vec_down,
            gain_one,
            shift_one,
            gain_two,
            shift_two,
        ) = gathered
        parents = leaf_parent[micro_index]
        query_info = path_info(device_index * BLK_DEV, BLK_DEV, block_len, parents)
        key_infos = [
            path_info((device_index - distance) * BLK_DEV, BLK_DEV, block_len, parents)
            for distance in range(tree_dev)
        ]
        lives = [distance <= tree_place for distance in range(tree_dev)]
        resid = tokens[micro_index].astype(jnp.float32)
        gain_one32 = gain_one.astype(jnp.float32)
        shift_one32 = shift_one.astype(jnp.float32)
        gain_two32 = gain_two.astype(jnp.float32)
        shift_two32 = shift_two.astype(jnp.float32)
        normed1 = layer_norm(resid, gain_one32, shift_one32)
        normed1_b = normed1.astype(jnp.bfloat16)
        query = (
            jnp.dot(normed1_b, mat_query, preferred_element_type=jnp.float32)
            + vec_query.astype(jnp.float32)
        ).astype(jnp.bfloat16)
        key = jnp.dot(normed1_b, mat_key, preferred_element_type=jnp.float32).astype(jnp.bfloat16)
        value = (
            jnp.dot(normed1_b, mat_value, preferred_element_type=jnp.float32)
            + vec_value.astype(jnp.float32)
        ).astype(jnp.bfloat16)
        query_h = query.reshape(row_count, head_count, head_dim)
        own_pair = jnp.stack((key, value))
        pairs = [own_pair]
        for distance in range(1, tree_dev):
            pairs.append(from_behind(own_pair, "dp", distance))
        key_heads = [pair[0].reshape(row_count, head_count, head_dim) for pair in pairs]
        value_heads = [pair[1].reshape(row_count, head_count, head_dim) for pair in pairs]
        scores = [
            scored(
                lives[distance],
                query_h,
                key_heads[distance],
                query_info,
                key_infos[distance],
                score_scale,
            )
            for distance in range(tree_dev)
        ]
        row_peak = jnp.max(scores[0], axis=-1)
        for block in scores[1:]:
            row_peak = jnp.maximum(row_peak, jnp.max(block, axis=-1))
        row_total = jnp.zeros_like(row_peak)
        for block in scores:
            row_total = row_total + jnp.sum(jnp.exp(block - row_peak[:, :, None]), axis=-1)
        log_total = row_peak + jnp.log(row_total)
        context = jnp.zeros((row_count, head_count, head_dim), jnp.float32)
        for distance in range(tree_dev):
            context = add_context(
                lives[distance], context, scores[distance], log_total, value_heads[distance]
            )
        context_b = context.reshape(row_count, feature_width).astype(jnp.bfloat16)
        attn = jnp.dot(context_b, mat_out, preferred_element_type=jnp.float32) + vec_out.astype(
            jnp.float32
        )
        middle = resid + attn
        normed2 = layer_norm(middle, gain_two32, shift_two32)
        normed2_b = normed2.astype(jnp.bfloat16)
        upper = jnp.dot(normed2_b, mat_up, preferred_element_type=jnp.float32) + vec_up.astype(
            jnp.float32
        )
        active_b = gelu_tanh(upper).astype(jnp.bfloat16)
        result = (
            middle
            + jnp.dot(active_b, mat_down, preferred_element_type=jnp.float32)
            + vec_down.astype(jnp.float32)
        )
        outputs.append(result.astype(jnp.bfloat16))
        backward_set = (
            lax.all_gather(w_query, "dp", axis=0, tiled=True),
            lax.all_gather(w_key, "dp", axis=0, tiled=True),
            lax.all_gather(w_value, "dp", axis=0, tiled=True),
            lax.all_gather(w_attn_out, "dp", axis=0, tiled=True),
            lax.all_gather(w_up, "dp", axis=0, tiled=True),
            lax.all_gather(w_down, "dp", axis=0, tiled=True),
            lax.all_gather(b_query, "dp", axis=0, tiled=True),
            lax.all_gather(b_value, "dp", axis=0, tiled=True),
            lax.all_gather(b_attn_out, "dp", axis=0, tiled=True),
            lax.all_gather(b_up, "dp", axis=0, tiled=True),
            lax.all_gather(b_down, "dp", axis=0, tiled=True),
            lax.all_gather(ln1_gain, "dp", axis=0, tiled=True),
            lax.all_gather(ln1_bias, "dp", axis=0, tiled=True),
            lax.all_gather(ln2_gain, "dp", axis=0, tiled=True),
            lax.all_gather(ln2_bias, "dp", axis=0, tiled=True),
        )
        back_query, back_key, back_value, back_out, back_up, back_down = backward_set[:6]
        back_gain_one = backward_set[11].astype(jnp.float32)
        back_gain_two = backward_set[13].astype(jnp.float32)
        grad_b = grad_out[micro_index]
        grad_y = grad_b.astype(jnp.float32)
        grad_down = jnp.einsum("tf,td->fd", active_b, grad_b, preferred_element_type=jnp.float32)
        grad_vec_down = jnp.sum(grad_y, axis=0)
        grad_active = jnp.einsum("td,fd->tf", grad_b, back_down, preferred_element_type=jnp.float32)
        gelu_value, gelu_pull = jax.vjp(gelu_tanh, upper)
        grad_upper_b = gelu_pull(grad_active)[0].astype(jnp.bfloat16)
        grad_up = jnp.einsum(
            "td,tf->df", normed2_b, grad_upper_b, preferred_element_type=jnp.float32
        )
        grad_vec_up = jnp.sum(grad_upper_b, axis=0, dtype=jnp.float32)
        grad_normed2 = jnp.einsum(
            "tf,df->td", grad_upper_b, back_up, preferred_element_type=jnp.float32
        )
        norm_value, norm_pull = jax.vjp(layer_norm, middle, back_gain_two, shift_two32)
        grad_mid_norm, grad_gain_two, grad_shift_two = norm_pull(grad_normed2)
        grad_middle = grad_y + grad_mid_norm
        grad_attn_b = grad_middle.astype(jnp.bfloat16)
        grad_out_mat = jnp.einsum(
            "td,te->de", context_b, grad_attn_b, preferred_element_type=jnp.float32
        )
        grad_vec_out = jnp.sum(grad_attn_b, axis=0, dtype=jnp.float32)
        grad_ctx_b = jnp.einsum(
            "te,de->td", grad_attn_b, back_out, preferred_element_type=jnp.float32
        ).astype(jnp.bfloat16)
        grad_ctx_h = grad_ctx_b.reshape(row_count, head_count, head_dim)
        prob_list = []
        grad_prob_list = []
        delta = jnp.zeros((head_count, row_count), jnp.float32)
        for distance in range(tree_dev):
            probs, grad_probs = prob_pair(
                lives[distance],
                query_h,
                key_heads[distance],
                value_heads[distance],
                grad_ctx_h,
                query_info,
                key_infos[distance],
                log_total,
                score_scale,
            )
            prob_list.append(probs)
            grad_prob_list.append(grad_probs)
            delta = delta + jnp.sum(probs * grad_probs, axis=-1)
        grad_query = jnp.zeros((row_count, head_count, head_dim), jnp.float32)
        pair_total = jnp.zeros((2, row_count, feature_width), jnp.float32)
        for distance in range(tree_dev):
            query_part, pair_part = block_back(
                lives[distance],
                prob_list[distance],
                grad_prob_list[distance],
                delta,
                query_h,
                key_heads[distance],
                grad_ctx_h,
                score_scale,
            )
            grad_query = grad_query + query_part
            if distance == 0:
                pair_total = pair_part
            else:
                pair_total = pair_total + from_behind(
                    pair_part.astype(jnp.bfloat16), "dp", -distance
                ).astype(pair_part.dtype)
        grad_query_b = grad_query.reshape(row_count, feature_width).astype(jnp.bfloat16)
        grad_key_b = pair_total[0].astype(jnp.bfloat16)
        grad_value_b = pair_total[1].astype(jnp.bfloat16)
        grad_query_mat = jnp.einsum(
            "td,te->de", normed1_b, grad_query_b, preferred_element_type=jnp.float32
        )
        grad_key_mat = jnp.einsum(
            "td,te->de", normed1_b, grad_key_b, preferred_element_type=jnp.float32
        )
        grad_value_mat = jnp.einsum(
            "td,te->de", normed1_b, grad_value_b, preferred_element_type=jnp.float32
        )
        grad_vec_query = jnp.sum(grad_query_b, axis=0, dtype=jnp.float32)
        grad_vec_value = jnp.sum(grad_value_b, axis=0, dtype=jnp.float32)
        grad_normed1 = jnp.einsum(
            "te,de->td", grad_query_b, back_query, preferred_element_type=jnp.float32
        )
        grad_normed1 = grad_normed1 + jnp.einsum(
            "te,de->td", grad_key_b, back_key, preferred_element_type=jnp.float32
        )
        grad_normed1 = grad_normed1 + jnp.einsum(
            "te,de->td", grad_value_b, back_value, preferred_element_type=jnp.float32
        )
        first_value, first_pull = jax.vjp(layer_norm, resid, back_gain_one, shift_one32)
        grad_res_norm, grad_gain_one, grad_shift_one = first_pull(grad_normed1)
        input_grads.append((grad_middle + grad_res_norm).astype(jnp.bfloat16))
        terms = (
            grad_query_mat,
            grad_key_mat,
            grad_value_mat,
            grad_out_mat,
            grad_up,
            grad_down,
            grad_vec_query,
            grad_vec_value,
            grad_vec_out,
            grad_vec_up,
            grad_vec_down,
            grad_gain_one,
            grad_shift_one,
            grad_gain_two,
            grad_shift_two,
        )
        totals = [accum + term for accum, term in zip(totals, terms)]
    sums = (
        lax.psum_scatter(totals[0], "dp", scatter_dimension=0, tiled=True),
        lax.psum_scatter(totals[1], "dp", scatter_dimension=0, tiled=True),
        lax.psum_scatter(totals[2], "dp", scatter_dimension=0, tiled=True),
        lax.psum_scatter(totals[3], "dp", scatter_dimension=0, tiled=True),
        lax.psum_scatter(totals[4], "dp", scatter_dimension=0, tiled=True),
        lax.psum_scatter(totals[5], "dp", scatter_dimension=0, tiled=True),
        lax.psum_scatter(totals[6], "dp", scatter_dimension=0, tiled=True),
        lax.psum_scatter(totals[7], "dp", scatter_dimension=0, tiled=True),
        lax.psum_scatter(totals[8], "dp", scatter_dimension=0, tiled=True),
        lax.psum_scatter(totals[9], "dp", scatter_dimension=0, tiled=True),
        lax.psum_scatter(totals[10], "dp", scatter_dimension=0, tiled=True),
        lax.psum_scatter(totals[11], "dp", scatter_dimension=0, tiled=True),
        lax.psum_scatter(totals[12], "dp", scatter_dimension=0, tiled=True),
        lax.psum_scatter(totals[13], "dp", scatter_dimension=0, tiled=True),
        lax.psum_scatter(totals[14], "dp", scatter_dimension=0, tiled=True),
    )
    return (
        jnp.stack(outputs),
        jnp.stack(input_grads),
        sums[0],
        sums[1],
        sums[2],
        sums[3],
        sums[4],
        sums[5],
        sums[6],
        sums[7],
        sums[8],
        sums[9],
        sums[10],
        sums[11],
        sums[12],
        sums[13],
        sums[14],
    )


def solution(mesh):
    placed = (
        P(None, "dp", None),
        P(None, "dp", None),
        P("dp", None),
        P("dp", None),
        P("dp", None),
        P("dp"),
        P("dp"),
        P("dp", None),
        P("dp"),
        P("dp", None),
        P("dp"),
        P("dp", None),
        P("dp"),
        P("dp"),
        P("dp"),
        P("dp"),
        P("dp"),
        P(),
    )
    return jax.shard_map(
        on_device,
        mesh=mesh,
        in_specs=placed,
        out_specs=(
            P(None, "dp", None),
            P(None, "dp", None),
            P("dp", None),
            P("dp", None),
            P("dp", None),
            P("dp", None),
            P("dp", None),
            P("dp", None),
            P("dp"),
            P("dp"),
            P("dp"),
            P("dp"),
            P("dp"),
            P("dp"),
            P("dp"),
            P("dp"),
            P("dp"),
        ),
        check_vma=False,
    )
```

profile of v0, /device:TPU:0, one launch (start us, length us, event | category | flops | bytes accessed | tf_op | source)
XLA Modules:
  0.0 1931.7 jit_solution(498743303622954952)
XLA Ops:
  18.0 42.4 %all-reduce.18 = (bf16[1024]{0:T(1024)(128)(2,1)S(1)}, bf16[1024]{0:T(1024)(128)(2,1)S(1)}, bf16[1024]{0:T(1024)(128)(2,1)S(1)}, bf16[1024]{0:T(1024)(128)(2,1)S...) all-reduce(bf16[1024]{0:T(1024)(128)(2,1)S(1)} %dynamic-update-slic, ...), channel_id=1, replica_groups=mesh['dp'=32] {'dp'}, use_global_device_ids=true, to_apply=%add.2 | all-reduce | flops 8192 | bytes 32768
  61.0 40.7 %all-gather = bf16[32,1,128]{2,1,0:T(2,128)(2,1)S(1)} all-gather(bf16[1,1,128]{2,1,0:T(2,128)(2,1)} %bitcast.482), channel_id=1, replica_groups=mesh['dp'=32] {'dp'}, dimensions={0}, use_global_device_ids=true | all-gather | bytes 8448 | tf_op jit(solution)/shard_map/all_gather | solution.py:230
  113.6 14.9 all-gather.12.cloned.1.call-done
  148.0 56.3 %all-gather.8.cloned.1.call-done = bf16[1024,1024]{1,0:T(8,128)(2,1)} async-done(((bf16[32,1024]{1,0:T(8,128)(2,1)}), bf16[1024,1024]{1,0:T(8,128)(2,1)}) %all-gather.8.cloned.1.call-update) | async-done | bytes 2097168 | tf_op jit(solution)/shard_map/all_gather | solution.py:221
  269.8 14.5 collective-permute-start.3
  313.6 9.0 exponential_reduce_fusion.6
  324.8 6.4 conditional.88
  344.2 26.3 %collective-permute-start.2 = (bf16[2,160,1024]{2,1,0:T(8,128)(2,1)}, bf16[2,160,1024]{2,1,0:T(8,128)(2,1)}, u32[]{:S(2)}, u32[]{:S(2)}) collective-permute-start(bf16[2,160,1024]{2,1,0:T(8,128)(2,1)} %pad_maximum_fusion.16), channel_id=1, source_target_pairs={{0,3},{1,4},{2,5},{3,6},{4,7},{5,8},{6,9},{7,10},{8,11},{9,12},{10... | collective-permute-start | bytes 1966088 | tf_op jit(solution)/shard_map/ppermute | solution.py:22
  373.8 23.9 %collective-permute-start.1 = (bf16[2,160,1024]{2,1,0:T(8,128)(2,1)}, bf16[2,160,1024]{2,1,0:T(8,128)(2,1)}, u32[]{:S(2)}, u32[]{:S(2)}) collective-permute-start(bf16[2,160,1024]{2,1,0:T(8,128)(2,1)} %pad_maximum_fusion.16), channel_id=1, source_target_pairs={{0,2},{1,3},{2,4},{3,5},{4,6},{5,7},{6,8},{7,9},{8,10},{9,11},{10,... | collective-permute-start | bytes 1966088 | tf_op jit(solution)/shard_map/ppermute | solution.py:22
  446.8 9.1 exponential_reduce_fusion.14
  457.4 7.0 conditional.72
  483.6 6.6 convolution_add_fusion.2
  493.5 8.8 convert_reduce_fusion
  503.4 6.4 fusion.446
  509.9 8.4 convert_reduce_fusion.1
  568.1 6.3 conditional.112
  626.3 6.6 conditional.96
  652.2 11.4 conditional.104
  681.5 11.8 conditional.120
  728.5 227.1 %collective-permute-done.27 = bf16[2,160,1024]{2,1,0:T(8,128)(2,1)} collective-permute-done((bf16[2,160,1024]{2,1,0:T(8,128)(2,1)}, bf16[2,160,1024]{2,1,0:T(8,128)(2,1)}, u32[]{:S(2)}, u32[]{:S(2)}) %collective-permute-start.27) | collective-permute-done | bytes 655392 | tf_op jit(solution)/shard_map/ppermute | solution.py:22
  958.2 15.1 collective-permute-done.20
  997.9 5.8 collective-permute-done.25
  1003.7 19.7 %collective-permute-done.24 = bf16[2,160,1024]{2,1,0:T(8,128)(2,1)S(1)} collective-permute-done((bf16[2,160,1024]{2,1,0:T(8,128)(2,1)}, bf16[2,160,1024]{2,1,0:T(8,128)(2,1)S(1)}, u32[]{:S(2)}, u32[]{:S(2)}) %collective-permute-start.24) | collective-permute-done | bytes 655392 | tf_op jit(solution)/shard_map/ppermute | solution.py:22
  1039.8 9.8 convolution_add_fusion.1
  1054.1 10.2 convolution_add_fusion
  1065.4 6.2 fusion.279
  1085.4 153.1 %all-reduce.17 = (f32[1024]{0:T(1024)S(1)}, f32[1024]{0:T(1024)S(1)}, f32[1024]{0:T(1024)S(1)}, f32[4096]{0:T(1024)S(1)}, f32[1024]{0:T(1024)S(1)}, /*index=5*/f...) all-reduce(f32[1024]{0:T(1024)S(1)} %add.1941, ...), channel_id=8, replica_groups=mesh['dp'=32] {'dp'}, use_global_device_ids=true, to_apply=%region_204.205.clone | all-reduce | flops 12288 | bytes 98304
  1246.8 29.1 %reduce-scatter.13.cloned.1.call-done = f32[32,1024]{1,0:T(8,128)} async-done(((f32[1024,1024]{1,0:T(8,128)}), f32[32,1024]{1,0:T(8,128)}) %reduce-scatter.13.cloned.1.call-update) | async-done | bytes 131088 | tf_op jit(solution)/shard_map/reduce_scatter | solution.py:456
  1275.9 140.1 %reduce-scatter.9.cloned.1.call-done = f32[32,1024]{1,0:T(8,128)} async-done(((f32[1024,1024]{1,0:T(8,128)}), f32[32,1024]{1,0:T(8,128)}) %reduce-scatter.9.cloned.1.call-update) | async-done | bytes 131088 | tf_op jit(solution)/shard_map/reduce_scatter | solution.py:454
  1416.0 139.6 %reduce-scatter.11.cloned.1.call-done = f32[32,1024]{1,0:T(8,128)} async-done(((f32[1024,1024]{1,0:T(8,128)}), f32[32,1024]{1,0:T(8,128)}) %reduce-scatter.11.cloned.1.call-update) | async-done | bytes 131088 | tf_op jit(solution)/shard_map/reduce_scatter | solution.py:455
  1555.7 181.7 %reduce-scatter.15.cloned.1.call-done = f32[32,4096]{1,0:T(8,128)} async-done(((f32[1024,4096]{1,0:T(8,128)}), f32[32,4096]{1,0:T(8,128)}) %reduce-scatter.15.cloned.1.call-update) | async-done | bytes 524304 | tf_op jit(solution)/shard_map/reduce_scatter | solution.py:457
  1737.3 187.1 %reduce-scatter.17.cloned.1.call-done = f32[128,1024]{1,0:T(8,128)} async-done(((f32[4096,1024]{1,0:T(8,128)}), f32[128,1024]{1,0:T(8,128)}) %reduce-scatter.17.cloned.1.call-update) | async-done | bytes 524304 | tf_op jit(solution)/shard_map/reduce_scatter | solution.py:458
  (868 shorter events, 616.0 us)
Async XLA Ops:
  7.2 104.2 %all-gather.10.cloned.1.call-start = ((), (), s32[]{:S(2)}) async-start(), calls=%async_computation.7 | async-start | bytes 2162688 | tf_op jit(solution)/shard_map/all_gather | solution.py:222
  7.9 120.6 %all-gather.12.cloned.1.call-start = ((), (), s32[]{:S(2)}) async-start(), calls=%async_computation.8 | async-start | bytes 2162688 | tf_op jit(solution)/shard_map/all_gather | solution.py:223
  8.7 195.6 %all-gather.8.cloned.1.call-start = ((), (), s32[]{:S(2)}) async-start(), calls=%async_computation.6 | async-start | bytes 2162688 | tf_op jit(solution)/shard_map/all_gather | solution.py:221
  9.4 469.6 %all-gather.14.cloned.1.call-start = ((), (), s32[]{:S(2)}) async-start(), calls=%async_computation.9 | async-start | bytes 2162688 | tf_op jit(solution)/shard_map/all_gather | solution.py:224
  10.0 473.5 %all-gather.16.cloned.1.call-start = ((), (), s32[]{:S(2)}) async-start(), calls=%async_computation.10 | async-start | bytes 8650752 | tf_op jit(solution)/shard_map/all_gather | solution.py:225
  10.6 482.9 %all-gather.18.cloned.1.call-start = ((), (), s32[]{:S(2)}) async-start(), calls=%async_computation.11 | async-start | bytes 8650752 | tf_op jit(solution)/shard_map/all_gather | solution.py:226
  11.2 1235.6 %reduce-scatter.7.cloned.1.call-start = ((), (), s32[]{:S(2)}) async-start(), calls=%async_computation.12 | async-start | bytes 4325376 | tf_op jit(solution)/shard_map/reduce_scatter | solution.py:453
  131.6 96.1 %collective-permute-start.7 = (bf16[2,160,1024]{2,1,0:T(8,128)(2,1)}, bf16[2,160,1024]{2,1,0:T(8,128)(2,1)}, u32[]{:S(2)}, u32[]{:S(2)}) collective-permute-start(bf16[2,160,1024]{2,1,0:T(8,128)(2,1)} %pad_maximum_fusion.17), channel_id=1, source_target_pairs={{0,1},{1,2},{2,3},{3,4},{4,5},{5,6},{6,7},{7,8},{8,9},{9,10},{10,1... | collective-permute-start | bytes 1966088 | tf_op jit(solution)/shard_map/ppermute | solution.py:22
  134.6 96.9 %collective-permute-start.13 = (bf16[2,160,1024]{2,1,0:T(8,128)(2,1)}, bf16[2,160,1024]{2,1,0:T(8,128)(2,1)}, u32[]{:S(2)}, u32[]{:S(2)}) collective-permute-start(bf16[2,160,1024]{2,1,0:T(8,128)(2,1)} %pad_maximum_fusion.17), channel_id=1, source_target_pairs={{0,7},{1,8},{2,9},{3,10},{4,11},{5,12},{6,13},{7,14},{8,15},{9,16}... | collective-permute-start | bytes 1966088 | tf_op jit(solution)/shard_map/ppermute | solution.py:22
  138.9 100.9 %collective-permute-start.12 = (bf16[2,160,1024]{2,1,0:T(8,128)(2,1)}, bf16[2,160,1024]{2,1,0:T(8,128)(2,1)}, u32[]{:S(2)}, u32[]{:S(2)}) collective-permute-start(bf16[2,160,1024]{2,1,0:T(8,128)(2,1)} %pad_maximum_fusion.17), channel_id=1, source_target_pairs={{0,6},{1,7},{2,8},{3,9},{4,10},{5,11},{6,12},{7,13},{8,14},{9,15},... | collective-permute-start | bytes 1966088 | tf_op jit(solution)/shard_map/ppermute | solution.py:22
  142.4 103.8 %collective-permute-start.11 = (bf16[2,160,1024]{2,1,0:T(8,128)(2,1)}, bf16[2,160,1024]{2,1,0:T(8,128)(2,1)}, u32[]{:S(2)}, u32[]{:S(2)}) collective-permute-start(bf16[2,160,1024]{2,1,0:T(8,128)(2,1)} %pad_maximum_fusion.17), channel_id=1, source_target_pairs={{0,5},{1,6},{2,7},{3,8},{4,9},{5,10},{6,11},{7,12},{8,13},{9,14},{... | collective-permute-start | bytes 1966088 | tf_op jit(solution)/shard_map/ppermute | solution.py:22
  144.8 110.0 %collective-permute-start.10 = (bf16[2,160,1024]{2,1,0:T(8,128)(2,1)}, bf16[2,160,1024]{2,1,0:T(8,128)(2,1)}, u32[]{:S(2)}, u32[]{:S(2)}) collective-permute-start(bf16[2,160,1024]{2,1,0:T(8,128)(2,1)} %pad_maximum_fusion.17), channel_id=1, source_target_pairs={{0,4},{1,5},{2,6},{3,7},{4,8},{5,9},{6,10},{7,11},{8,12},{9,13},{1... | collective-permute-start | bytes 1966088 | tf_op jit(solution)/shard_map/ppermute | solution.py:22
  231.5 38.4 %collective-permute-start.8 = (bf16[2,160,1024]{2,1,0:T(8,128)(2,1)}, bf16[2,160,1024]{2,1,0:T(8,128)(2,1)}, u32[]{:S(2)}, u32[]{:S(2)}) collective-permute-start(bf16[2,160,1024]{2,1,0:T(8,128)(2,1)} %pad_maximum_fusion.17), channel_id=1, source_target_pairs={{0,2},{1,3},{2,4},{3,5},{4,6},{5,7},{6,8},{7,9},{8,10},{9,11},{10,... | collective-permute-start | bytes 1966088 | tf_op jit(solution)/shard_map/ppermute | solution.py:22
  239.8 104.4 %collective-permute-start = (bf16[2,160,1024]{2,1,0:T(8,128)(2,1)}, bf16[2,160,1024]{2,1,0:T(8,128)(2,1)}, u32[]{:S(2)}, u32[]{:S(2)}) collective-permute-start(bf16[2,160,1024]{2,1,0:T(8,128)(2,1)} %pad_maximum_fusion.16), channel_id=1, source_target_pairs={{0,1},{1,2},{2,3},{3,4},{4,5},{5,6},{6,7},{7,8},{8,9},{9,10},{10,1... | collective-permute-start | bytes 1966088 | tf_op jit(solution)/shard_map/ppermute | solution.py:22
  246.2 127.6 %collective-permute-start.6 = (bf16[2,160,1024]{2,1,0:T(8,128)(2,1)}, bf16[2,160,1024]{2,1,0:T(8,128)(2,1)}, u32[]{:S(2)}, u32[]{:S(2)}) collective-permute-start(bf16[2,160,1024]{2,1,0:T(8,128)(2,1)} %pad_maximum_fusion.16), channel_id=1, source_target_pairs={{0,7},{1,8},{2,9},{3,10},{4,11},{5,12},{6,13},{7,14},{8,15},{9,16}... | collective-permute-start | bytes 1966088 | tf_op jit(solution)/shard_map/ppermute | solution.py:22
  254.7 147.3 %collective-permute-start.5 = (bf16[2,160,1024]{2,1,0:T(8,128)(2,1)}, bf16[2,160,1024]{2,1,0:T(8,128)(2,1)}, u32[]{:S(2)}, u32[]{:S(2)}) collective-permute-start(bf16[2,160,1024]{2,1,0:T(8,128)(2,1)} %pad_maximum_fusion.16), channel_id=1, source_target_pairs={{0,6},{1,7},{2,8},{3,9},{4,10},{5,11},{6,12},{7,13},{8,14},{9,15},... | collective-permute-start | bytes 1966088 | tf_op jit(solution)/shard_map/ppermute | solution.py:22
  262.2 144.1 %collective-permute-start.4 = (bf16[2,160,1024]{2,1,0:T(8,128)(2,1)}, bf16[2,160,1024]{2,1,0:T(8,128)(2,1)}, u32[]{:S(2)}, u32[]{:S(2)}) collective-permute-start(bf16[2,160,1024]{2,1,0:T(8,128)(2,1)} %pad_maximum_fusion.16), channel_id=1, source_target_pairs={{0,5},{1,6},{2,7},{3,8},{4,9},{5,10},{6,11},{7,12},{8,13},{9,14},{... | collective-permute-start | bytes 1966088 | tf_op jit(solution)/shard_map/ppermute | solution.py:22
  269.8 140.6 %collective-permute-start.3 = (bf16[2,160,1024]{2,1,0:T(8,128)(2,1)}, bf16[2,160,1024]{2,1,0:T(8,128)(2,1)}, u32[]{:S(2)}, u32[]{:S(2)}) collective-permute-start(bf16[2,160,1024]{2,1,0:T(8,128)(2,1)} %pad_maximum_fusion.16), channel_id=1, source_target_pairs={{0,4},{1,5},{2,6},{3,7},{4,8},{5,9},{6,10},{7,11},{8,12},{9,13},{1... | collective-permute-start | bytes 1966088 | tf_op jit(solution)/shard_map/ppermute | solution.py:22
  344.2 70.5 %collective-permute-start.2 = (bf16[2,160,1024]{2,1,0:T(8,128)(2,1)}, bf16[2,160,1024]{2,1,0:T(8,128)(2,1)}, u32[]{:S(2)}, u32[]{:S(2)}) collective-permute-start(bf16[2,160,1024]{2,1,0:T(8,128)(2,1)} %pad_maximum_fusion.16), channel_id=1, source_target_pairs={{0,3},{1,4},{2,5},{3,6},{4,7},{5,8},{6,9},{7,10},{8,11},{9,12},{10... | collective-permute-start | bytes 1966088 | tf_op jit(solution)/shard_map/ppermute | solution.py:22
  373.8 45.2 %collective-permute-start.1 = (bf16[2,160,1024]{2,1,0:T(8,128)(2,1)}, bf16[2,160,1024]{2,1,0:T(8,128)(2,1)}, u32[]{:S(2)}, u32[]{:S(2)}) collective-permute-start(bf16[2,160,1024]{2,1,0:T(8,128)(2,1)} %pad_maximum_fusion.16), channel_id=1, source_target_pairs={{0,2},{1,3},{2,4},{3,5},{4,6},{5,7},{6,8},{7,9},{8,10},{9,11},{10,... | collective-permute-start | bytes 1966088 | tf_op jit(solution)/shard_map/ppermute | solution.py:22
  702.4 573.6 %reduce-scatter.13.cloned.1.call-start = ((), (), s32[]{:S(2)}) async-start(), calls=%async_computation.15 | async-start | bytes 4325376 | tf_op jit(solution)/shard_map/reduce_scatter | solution.py:456
  706.9 709.1 %reduce-scatter.9.cloned.1.call-start = ((), (), s32[]{:S(2)}) async-start(), calls=%async_computation.13 | async-start | bytes 4325376 | tf_op jit(solution)/shard_map/reduce_scatter | solution.py:454
  709.2 246.3 %collective-permute-start.27 = (bf16[2,160,1024]{2,1,0:T(8,128)(2,1)}, bf16[2,160,1024]{2,1,0:T(8,128)(2,1)}, u32[]{:S(2)}, u32[]{:S(2)}) collective-permute-start(bf16[2,160,1024]{2,1,0:T(8,128)(2,1)} %copy.770), channel_id=1, source_target_pairs={{7,0},{8,1},{9,2},{10,3},{11,4},{12,5},{13,6},{14,7},{15,8},{16,9}... | collective-permute-start | bytes 1966088 | tf_op jit(solution)/shard_map/ppermute | solution.py:22
  712.7 244.2 %collective-permute-start.26 = (bf16[2,160,1024]{2,1,0:T(8,128)(2,1)}, bf16[2,160,1024]{2,1,0:T(8,128)(2,1)}, u32[]{:S(2)}, u32[]{:S(2)}) collective-permute-start(bf16[2,160,1024]{2,1,0:T(8,128)(2,1)} %copy.769), channel_id=1, source_target_pairs={{6,0},{7,1},{8,2},{9,3},{10,4},{11,5},{12,6},{13,7},{14,8},{15,9},... | collective-permute-start | bytes 1966088 | tf_op jit(solution)/shard_map/ppermute | solution.py:22
  715.2 258.1 %collective-permute-start.20 = (bf16[2,160,1024]{2,1,0:T(8,128)(2,1)}, bf16[2,160,1024]{2,1,0:T(8,128)(2,1)}, u32[]{:S(2)}, u32[]{:S(2)}) collective-permute-start(bf16[2,160,1024]{2,1,0:T(8,128)(2,1)} %copy.706), channel_id=1, source_target_pairs={{7,0},{8,1},{9,2},{10,3},{11,4},{12,5},{13,6},{14,7},{15,8},{16,9}... | collective-permute-start | bytes 1966088 | tf_op jit(solution)/shard_map/ppermute | solution.py:22
  717.8 256.7 %collective-permute-start.19 = (bf16[2,160,1024]{2,1,0:T(8,128)(2,1)}, bf16[2,160,1024]{2,1,0:T(8,128)(2,1)}, u32[]{:S(2)}, u32[]{:S(2)}) collective-permute-start(bf16[2,160,1024]{2,1,0:T(8,128)(2,1)} %copy.705), channel_id=1, source_target_pairs={{6,0},{7,1},{8,2},{9,3},{10,4},{11,5},{12,6},{13,7},{14,8},{15,9},... | collective-permute-start | bytes 1966088 | tf_op jit(solution)/shard_map/ppermute | solution.py:22
  721.4 261.7 %collective-permute-start.18 = (bf16[2,160,1024]{2,1,0:T(8,128)(2,1)}, bf16[2,160,1024]{2,1,0:T(8,128)(2,1)}, u32[]{:S(2)}, u32[]{:S(2)}) collective-permute-start(bf16[2,160,1024]{2,1,0:T(8,128)(2,1)} %copy.704), channel_id=1, source_target_pairs={{5,0},{6,1},{7,2},{8,3},{9,4},{10,5},{11,6},{12,7},{13,8},{14,9},{... | collective-permute-start | bytes 1966088 | tf_op jit(solution)/shard_map/ppermute | solution.py:22
  987.9 35.5 %collective-permute-start.24 = (bf16[2,160,1024]{2,1,0:T(8,128)(2,1)}, bf16[2,160,1024]{2,1,0:T(8,128)(2,1)S(1)}, u32[]{:S(2)}, u32[]{:S(2)}) collective-permute-start(bf16[2,160,1024]{2,1,0:T(8,128)(2,1)} %copy.767), channel_id=1, source_target_pairs={{4,0},{5,1},{6,2},{7,3},{8,4},{9,5},{10,6},{11,7},{12,8},{13,9},{1... | collective-permute-start | bytes 1966088 | tf_op jit(solution)/shard_map/ppermute | solution.py:22
  990.5 34.8 %collective-permute-start.22 = (bf16[2,160,1024]{2,1,0:T(8,128)(2,1)}, bf16[2,160,1024]{2,1,0:T(8,128)(2,1)S(1)}, u32[]{:S(2)}, u32[]{:S(2)}) collective-permute-start(bf16[2,160,1024]{2,1,0:T(8,128)(2,1)} %copy.765), channel_id=1, source_target_pairs={{2,0},{3,1},{4,2},{5,3},{6,4},{7,5},{8,6},{9,7},{10,8},{11,9},{12,... | collective-permute-start | bytes 1966088 | tf_op jit(solution)/shard_map/ppermute | solution.py:22
  1031.0 524.6 %reduce-scatter.11.cloned.1.call-start = ((), (), s32[]{:S(2)}) async-start(), calls=%async_computation.14 | async-start | bytes 4325376 | tf_op jit(solution)/shard_map/reduce_scatter | solution.py:455
  1034.9 702.4 %reduce-scatter.15.cloned.1.call-start = ((), (), s32[]{:S(2)}) async-start(), calls=%async_computation.16 | async-start | bytes 17301504 | tf_op jit(solution)/shard_map/reduce_scatter | solution.py:457
  1049.5 874.9 %reduce-scatter.17.cloned.1.call-start = ((), (), s32[]{:S(2)}) async-start(), calls=%async_computation.17 | async-start | bytes 17301504 | tf_op jit(solution)/shard_map/reduce_scatter | solution.py:458
  (186 other events, 4671.6 us)
Sparse Core Ops, SparseCore 0:
  10.9 59.4 all-gather.9
  73.2 55.2 all-gather.11
  131.3 72.8 all-gather.7
  207.0 67.0 all-gather.13
  276.7 92.0 all-gather.15
  371.6 94.8 all-gather.17
  702.5 431.0 reduce-scatter.6
  1136.4 139.5 reduce-scatter.12
  1278.8 137.2 reduce-scatter.8
  1418.7 136.8 reduce-scatter.10
  1558.5 178.7 reduce-scatter.14
  1740.0 184.3 reduce-scatter.16
where the time goes:
time: 1950 us; the launch traced here: 1930 us
  waiting for transfers between devices  1030 us (53%)
  local copies, waits for them, and re-layouts  266 us (14%)
  blocking collectives  236 us (12%)
  matrix products  148 us (8%)
  starting transfers between devices  120 us (6%)
  other arithmetic  115 us (6%)
    ppermute x28, waiting for transfers between devices, from_behind(): lax.ppermute(value, axis, [(source, source + steps) for source in range(l...  273 us
    unnamed x2, blocking collectives  195 us
    reduce_scatter x1, waiting for transfers between devices, on_device(): lax.psum_scatter(totals[5], 'dp', scatter_dimension=0, tiled=True)  187 us
    reduce_scatter x1, waiting for transfers between devices, on_device(): lax.psum_scatter(totals[4], 'dp', scatter_dimension=0, tiled=True)  182 us
    reduce_scatter x1, waiting for transfers between devices, on_device(): lax.psum_scatter(totals[1], 'dp', scatter_dimension=0, tiled=True)  140 us
    reduce_scatter x1, waiting for transfers between devices, on_device(): lax.psum_scatter(totals[2], 'dp', scatter_dimension=0, tiled=True)  140 us
    ppermute x28, starting transfers between devices, from_behind(): lax.ppermute(value, axis, [(source, source + steps) for source in range(l...  119 us
    another operation x72, local copies, waits for them, and re-layouts  84.1 us
  transfers between devices with their start and end apart: 40, of which 13 were waited for; matrix products, arithmetic and copies ran while one was open for 16% of the time, Pallas kernels for 0%

commit v1 on v0

v1 whole, which is shorter than its diff:
```python
from functools import partial

import jax
import jax.numpy as jnp
from jax import lax
from jax.experimental import pallas as pl
from jax.experimental.pallas import tpu as pltpu
from jax.sharding import PartitionSpec as P

HEADS = 16
BLK = 32
TRUNK_BLK = 16
SEG_BLK = 2
BRANCHES = 4
LEAVES = 8
TREE_BLK = 40

GROUP = 8
TREE = TREE_BLK * BLK
TRUNK = TRUNK_BLK * BLK
SEG = SEG_BLK * BLK
ROWS = 256
HALF = 128
HID = 64
NEG = -1e30

eps = 1e-05
bf16 = jnp.bfloat16
f32 = jnp.float32

FIRST = (2, 4)
SECOND = (4, 2)


def swap(value, mask):
    count = lax.axis_size("dp")
    return lax.ppermute(value, "dp", [(source, source ^ mask) for source in range(count)])


def plane_gather(own):
    near = [swap(own[m], FIRST[m]) for m in range(2)]
    pair = [jnp.stack((own[m], near[m])) for m in range(2)]
    far = [swap(pair[m], SECOND[m]) for m in range(2)]
    odd_a = [swap(pair[m], 1) for m in range(2)]
    odd_b = [swap(far[m], 1) for m in range(2)]
    return [
        (jnp.concatenate((pair[m], far[m])), jnp.concatenate((odd_a[m], odd_b[m])))
        for m in range(2)
    ]


def plane_scatter(even, odd):
    back = [swap(odd[m].astype(bf16), 1) for m in range(2)]
    total = [even[m].astype(f32) + back[m].astype(f32) for m in range(2)]
    far = [swap(total[m][2:].astype(bf16), SECOND[m]) for m in range(2)]
    pair = [total[m][:2] + far[m].astype(f32) for m in range(2)]
    near = [swap(pair[m][1].astype(bf16), FIRST[m]) for m in range(2)]
    return [pair[m][0] + near[m].astype(f32) for m in range(2)]


def plane_groups():
    count = lax.axis_size("dp")
    return [list(range(first, first + GROUP)) for first in range(0, count, GROUP)]


def column_groups():
    count = lax.axis_size("dp")
    return [list(range(place, count, GROUP)) for place in range(GROUP)]


def plane_exchange(value):
    return lax.all_to_all(value, "dp", 0, 0, tiled=True, axis_index_groups=plane_groups())


def column_gather(value, column_place):
    planes = lax.axis_size("dp") // GROUP
    if planes > 4:
        return lax.all_gather(value, "dp", axis=0, axis_index_groups=column_groups())
    parts = jnp.stack([value] + [swap(value, GROUP * step) for step in range(1, planes)])
    return jnp.stack(
        [
            lax.dynamic_index_in_dim(parts, column_place ^ plane, 0, keepdims=False)
            for plane in range(planes)
        ]
    )


def column_scatter(value, column_place):
    planes = lax.axis_size("dp") // GROUP
    if planes > 4:
        return lax.psum_scatter(
            value, "dp", scatter_dimension=0, axis_index_groups=column_groups()
        )
    total = lax.dynamic_index_in_dim(value, column_place, 0, keepdims=False)
    for step in range(1, planes):
        part = lax.dynamic_index_in_dim(value, column_place ^ step, 0, keepdims=False)
        total = total + swap(part.astype(bf16), GROUP * step).astype(f32)
    return total


def layer_norm_parts(values):
    center = values - jnp.mean(values, axis=-1, keepdims=True)
    spread = jnp.mean(center * center, axis=-1, keepdims=True)
    scale = lax.rsqrt(spread + eps)
    return center * scale, scale


def layer_norm_back(grad, unit, scale, gain):
    scaled = grad * gain
    return scale * (
        scaled
        - jnp.mean(scaled, axis=-1, keepdims=True)
        - unit * jnp.mean(scaled * unit, axis=-1, keepdims=True)
    )


def gelu_tanh(values):
    return jax.nn.gelu(values, approximate=True)


def mm(left, right, contract):
    return lax.dot_general(left, right, (contract, ((), ())), preferred_element_type=f32)


NN = ((1,), (0,))
NT = ((1,), (1,))
TN = ((0,), (0,))


def split3(values):
    high = values.astype(bf16)
    rest = values - high.astype(f32)
    middle = rest.astype(bf16)
    low = (rest - middle.astype(f32)).astype(bf16)
    return high, middle, low


def key_positions():
    row = lax.broadcasted_iota(jnp.int32, (TREE, 128), 0)
    after = row - TRUNK
    return jnp.where(
        row < TRUNK,
        row,
        jnp.where(
            after < BRANCHES * SEG, TRUNK + (after & (SEG - 1)), TRUNK + SEG + (after & (SEG - 1))
        ),
    )


def load_tree(order_ref, packed_ref, query_s, key_s, slope_ref, micro):
    lane = lax.broadcasted_iota(jnp.int32, (TREE, 128), 1)
    rows = TREE // GROUP
    for block in range(GROUP):
        part = packed_ref[0, order_ref[micro, block]]
        at = pl.ds(block * rows, rows)
        query_s[0, at, :] = part[:, 0:128]
        key_s[0, at, :] = part[:, 128:256]
    query = query_s[0] * jnp.asarray(0.125, bf16)
    key = key_s[0]
    place = key_positions().astype(f32)
    one = jnp.ones((TREE, 128), bf16)
    zero = jnp.zeros((TREE, 128), bf16)
    for head in range(2):
        mine = (lane < HID) if head == 0 else (lane >= HID)
        base = HID if head == 0 else 0
        high, middle, low = split3(place * slope_ref[head])
        extra = jnp.where(
            lane == base,
            high,
            jnp.where(lane == base + 1, middle, jnp.where(lane == base + 2, low, zero)),
        )
        ones = jnp.where((lane >= base) & (lane < base + 3), one, zero)
        query_s[head] = jnp.where(mine, query, ones)
        key_s[head] = jnp.where(mine, key, extra)


def tile_masks():
    row = lax.broadcasted_iota(jnp.int32, (HALF, HALF), 1)
    col = lax.broadcasted_iota(jnp.int32, (HALF, HALF), 0)
    same = (row // SEG) == (col // SEG)
    segment = jnp.where(same & (col <= row), 0.0, NEG)
    parent = jnp.where(same, 0.0, NEG)
    trow = lax.broadcasted_iota(jnp.int32, (ROWS, ROWS), 1)
    tcol = lax.broadcasted_iota(jnp.int32, (ROWS, ROWS), 0)
    causal = jnp.where(tcol <= trow, 0.0, NEG)
    return segment, parent, causal


def parent_rows(parent_ref, micro, leaf):
    start = TRUNK + (parent_ref[micro, leaf] - 1) * SEG
    return pl.ds(pl.multiple_of(start, SEG), SEG)


def tile_pieces(tile):
    if tile < TRUNK // ROWS:
        return (tile + 1) * ROWS, True, [], []
    start = tile * ROWS
    own = [start, start + HALF]
    first_leaf = TRUNK + BRANCHES * SEG
    leaves = []
    if start >= first_leaf:
        leaf = (start - first_leaf) // SEG
        leaves = [(leaf, leaf + 1), (leaf + 2, leaf + 3)]
    return TRUNK, False, own, leaves


def tile_scores(tile, key_ref, query, parent_ref, micro, masks, side):
    segment, parent, causal = masks
    trunk, last, own, leaves = tile_pieces(tile)
    scores = mm(key_ref[0:trunk, :], query, NT)
    pieces = []
    if last:
        if trunk > ROWS:
            pieces.append(scores[: trunk - ROWS])
        pieces.append(scores[trunk - ROWS :] + causal)
    else:
        pieces.append(scores)
    if own:
        pieces.append(
            jnp.concatenate(
                [
                    mm(key_ref[at : at + HALF, :], query[i * HALF : (i + 1) * HALF], NT) + segment
                    for i, at in enumerate(own)
                ],
                axis=1,
            )
        )
    if leaves:
        pieces.append(
            jnp.concatenate(
                [
                    mm(rows, query[i * HALF : (i + 1) * HALF], NT) + parent
                    for i, rows in enumerate(side)
                ],
                axis=1,
            )
        )
    return pieces


def forward_kernel(
    order_ref, parent_ref, slope_ref, packed_ref, ctx_ref, log_ref, query_s, key_s, value_s
):
    micro = pl.program_id(0)
    rows = TREE // GROUP
    load_tree(order_ref, packed_ref, query_s, key_s, slope_ref, micro)
    for block in range(GROUP):
        value_s[pl.ds(block * rows, rows), :] = packed_ref[0, order_ref[micro, block]][:, 256:384]
    masks = tile_masks()
    for tile in range(TREE // ROWS):
        trunk, last, own, leaves = tile_pieces(tile)
        at = slice(tile * ROWS, (tile + 1) * ROWS)
        contexts = []
        side_values = [
            jnp.concatenate([value_s[parent_rows(parent_ref, micro, leaf), :] for leaf in pair])
            for pair in leaves
        ]
        for head in range(2):
            query = query_s[head, at, :]
            side = [
                jnp.concatenate(
                    [key_s[head, parent_rows(parent_ref, micro, leaf), :] for leaf in pair]
                )
                for pair in leaves
            ]
            pieces = tile_scores(tile, key_s.at[head], query, parent_ref, micro, masks, side)
            peak = pieces[0].max(axis=0, keepdims=True)
            for piece in pieces[1:]:
                peak = jnp.maximum(peak, piece.max(axis=0, keepdims=True))
            probs = [jnp.exp(piece - peak) for piece in pieces]
            total = probs[0].sum(axis=0, keepdims=True)
            for piece in probs[1:]:
                total = total + piece.sum(axis=0, keepdims=True)
            probs = [piece.astype(bf16) for piece in probs]
            ntrunk = len(probs) - bool(own) - bool(leaves)
            context = jnp.zeros((128, ROWS), f32)
            start = 0
            for piece in probs[:ntrunk]:
                context = context + mm(value_s[start : start + piece.shape[0], :], piece, TN)
                start += piece.shape[0]
            if own:
                context = context + jnp.concatenate(
                    [
                        mm(
                            value_s[first : first + HALF, :],
                            probs[ntrunk][:, i * HALF : (i + 1) * HALF],
                            TN,
                        )
                        for i, first in enumerate(own)
                    ],
                    axis=1,
                )
            if leaves:
                context = context + jnp.concatenate(
                    [
                        mm(
                            side_values[i],
                            probs[ntrunk + 1][:, i * HALF : (i + 1) * HALF],
                            TN,
                        )
                        for i in range(2)
                    ],
                    axis=1,
                )
            half = slice(head * HID, (head + 1) * HID)
            contexts.append(context[half] / total)
            log_ref[0, head : head + 1, at] = peak + jnp.log(total)
        merged = jnp.concatenate(contexts, axis=0).T.astype(bf16)
        query_s[0, at, :] = merged
    for block in range(GROUP):
        ctx_ref[block, 0] = query_s[0, block * rows : (block + 1) * rows, :]


def backward_kernel(
    order_ref,
    parent_ref,
    slope_ref,
    packed_ref,
    ctx_ref,
    grad_ref,
    log_ref,
    out_ref,
    query_s,
    key_s,
    value_s,
    grad_s,
    dkey_s,
    dvalue_s,
    dquery_s,
):
    micro = pl.program_id(0)
    rows = TREE // GROUP
    load_tree(order_ref, packed_ref, query_s, key_s, slope_ref, micro)
    lane = lax.broadcasted_iota(jnp.int32, (rows, 128), 1)
    zero = jnp.zeros((rows, 128), bf16)
    for block in range(GROUP):
        at = pl.ds(block * rows, rows)
        value = packed_ref[0, order_ref[micro, block]][:, 256:384]
        grad = grad_ref[block, 0]
        for head in range(2):
            mine = (lane < HID) if head == 0 else (lane >= HID)
            value_s[head, at, :] = jnp.where(mine, value, zero)
            grad_s[head, at, :] = jnp.where(mine, grad, zero)
        dquery_s[at, :] = grad.astype(f32) * ctx_ref[block, 0].astype(f32)
    dkey_s[...] = jnp.zeros_like(dkey_s)
    dvalue_s[...] = jnp.zeros_like(dvalue_s)
    masks = tile_masks()
    for tile in range(TREE // ROWS):
        trunk, last, own, leaves = tile_pieces(tile)
        at = slice(tile * ROWS, (tile + 1) * ROWS)
        deltas = dquery_s[at, :].T
        dqueries = []
        for head in range(2):
            half = slice(head * HID, (head + 1) * HID)
            query = query_s[head, at, :]
            grad = grad_s[head, at, :]
            keys = key_s.at[head]
            values = value_s.at[head]
            side = [
                jnp.concatenate(
                    [key_s[head, parent_rows(parent_ref, micro, leaf), :] for leaf in pair]
                )
                for pair in leaves
            ]
            pieces = tile_scores(tile, keys, query, parent_ref, micro, masks, side)
            level = log_ref[0, head : head + 1, at]
            delta = deltas[half].sum(axis=0, keepdims=True)
            ntrunk = len(pieces) - bool(own) - bool(leaves)
            dquery = jnp.zeros((128, ROWS), f32)
            start = 0
            for piece in pieces[:ntrunk]:
                size = piece.shape[0]
                span = slice(start, start + size)
                probs = jnp.exp(piece - level)
                dprobs = mm(values[span, :], grad, NT)
                dscores = (probs * (dprobs - delta)).astype(bf16)
                dvalue_s[span, :] += mm(probs.astype(bf16), grad, NN)
                dkey_s[head, span, :] += mm(dscores, query, NN)
                dquery = dquery + mm(keys[span, :], dscores, TN)
                start += size
            extra = []
            for i, first in enumerate(own):
                cols = slice(i * HALF, (i + 1) * HALF)
                span = slice(first, first + HALF)
                probs = jnp.exp(pieces[ntrunk][:, cols] - level[:, cols])
                dprobs = mm(values[span, :], grad[cols], NT)
                dscores = (probs * (dprobs - delta[:, cols])).astype(bf16)
                dvalue_s[span, :] += mm(probs.astype(bf16), grad[cols], NN)
                dkey_s[head, span, :] += mm(dscores, query[cols], NN)
                extra.append(mm(keys[span, :], dscores, TN))
            if own:
                dquery = dquery + jnp.concatenate(extra, axis=1)
            extra = []
            for i, pair in enumerate(leaves):
                cols = slice(i * HALF, (i + 1) * HALF)
                side_value = jnp.concatenate(
                    [value_s[head, parent_rows(parent_ref, micro, leaf), :] for leaf in pair]
                )
                probs = jnp.exp(pieces[ntrunk + 1][:, cols] - level[:, cols])
                dprobs = mm(side_value, grad[cols], NT)
                dscores = (probs * (dprobs - delta[:, cols])).astype(bf16)
                dval = mm(probs.astype(bf16), grad[cols], NN)
                dkey = mm(dscores, query[cols], NN)
                for j, leaf in enumerate(pair):
                    span = parent_rows(parent_ref, micro, leaf)
                    dvalue_s[span, :] += dval[j * SEG : (j + 1) * SEG]
                    dkey_s[head, span, :] += dkey[j * SEG : (j + 1) * SEG]
                extra.append(mm(side[i], dscores, TN))
            if leaves:
                dquery = dquery + jnp.concatenate(extra, axis=1)
            dqueries.append(dquery[half] * 0.125)
        dquery_s[at, :] = jnp.concatenate(dqueries, axis=0).T
    for block in range(GROUP):
        at = slice(block * rows, (block + 1) * rows)
        slot = order_ref[micro, block]
        dkey = jnp.where(lane < HID, dkey_s[0, at, :], dkey_s[1, at, :])
        out_ref[0, slot] = jnp.concatenate(
            (dquery_s[at, :].astype(bf16), dkey.astype(bf16), dvalue_s[at, :].astype(bf16)), axis=1
        )


def attention_forward(order, parents, slopes, packed):
    micro_count, _, rows, width = packed.shape
    return pl.pallas_call(
        forward_kernel,
        out_shape=(
            jax.ShapeDtypeStruct((GROUP, micro_count, rows, 128), bf16),
            jax.ShapeDtypeStruct((micro_count, 8, TREE), f32),
        ),
        grid_spec=pltpu.PrefetchScalarGridSpec(
            num_scalar_prefetch=3,
            grid=(micro_count,),
            in_specs=[pl.BlockSpec((1, GROUP, rows, width), lambda m, *_: (m, 0, 0, 0))],
            out_specs=(
                pl.BlockSpec((GROUP, 1, rows, 128), lambda m, *_: (0, m, 0, 0)),
                pl.BlockSpec((1, 8, TREE), lambda m, *_: (m, 0, 0)),
            ),
            scratch_shapes=[
                pltpu.VMEM((2, TREE, 128), bf16),
                pltpu.VMEM((2, TREE, 128), bf16),
                pltpu.VMEM((TREE, 128), bf16),
            ],
        ),
        compiler_params=pltpu.CompilerParams(vmem_limit_bytes=40 << 20),
        cost_estimate=pl.CostEstimate(
            flops=4_000_000_000, transcendentals=3_000_000, bytes_accessed=3_000_000
        ),
        name="tree_attention",
    )(order, parents, slopes, packed)


def attention_backward(order, parents, slopes, packed, ctx, grad, logs):
    micro_count, _, rows, width = packed.shape
    return pl.pallas_call(
        backward_kernel,
        out_shape=jax.ShapeDtypeStruct(packed.shape, bf16),
        grid_spec=pltpu.PrefetchScalarGridSpec(
            num_scalar_prefetch=3,
            grid=(micro_count,),
            in_specs=[
                pl.BlockSpec((1, GROUP, rows, width), lambda m, *_: (m, 0, 0, 0)),
                pl.BlockSpec((GROUP, 1, rows, 128), lambda m, *_: (0, m, 0, 0)),
                pl.BlockSpec((GROUP, 1, rows, 128), lambda m, *_: (0, m, 0, 0)),
                pl.BlockSpec((1, 8, TREE), lambda m, *_: (m, 0, 0)),
            ],
            out_specs=pl.BlockSpec((1, GROUP, rows, width), lambda m, *_: (m, 0, 0, 0)),
            scratch_shapes=[
                pltpu.VMEM((2, TREE, 128), bf16),
                pltpu.VMEM((2, TREE, 128), bf16),
                pltpu.VMEM((2, TREE, 128), bf16),
                pltpu.VMEM((2, TREE, 128), bf16),
                pltpu.VMEM((2, TREE, 128), f32),
                pltpu.VMEM((TREE, 128), f32),
                pltpu.VMEM((TREE, 128), f32),
            ],
        ),
        compiler_params=pltpu.CompilerParams(vmem_limit_bytes=48 << 20),
        cost_estimate=pl.CostEstimate(
            flops=10_000_000_000, transcendentals=3_000_000, bytes_accessed=6_000_000
        ),
        name="tree_attention_back",
    )(order, parents, slopes, packed, ctx, grad, logs)


def on_device(
    tokens,
    grad_out,
    w_query,
    w_key,
    w_value,
    b_query,
    b_value,
    w_attn_out,
    b_attn_out,
    w_up,
    b_up,
    w_down,
    b_down,
    ln1_gain,
    ln1_bias,
    ln2_gain,
    ln2_bias,
    leaf_parent,
):
    micro_count, row_count, width = tokens.shape
    count = lax.axis_size("dp")
    planes = count // GROUP
    index = lax.axis_index("dp")
    place = index % GROUP
    plane = index // GROUP
    wrow = w_query.shape[0]
    frow = w_down.shape[0]
    head_width = width // GROUP
    unit_width = planes * frow
    both = range(micro_count)

    gathered_x = plane_gather([tokens[m] for m in both])

    def by_place(weight, shape):
        return weight.reshape(shape)

    packed_w = jnp.concatenate(
        [w.reshape(wrow, GROUP, head_width) for w in (w_query, w_key, w_value)], axis=2
    ).transpose(1, 0, 2)
    up_w = w_up.reshape(wrow, planes, GROUP, frow).transpose(2, 0, 1, 3)
    up_w = up_w.reshape(GROUP, wrow, unit_width)
    small = (b_query, b_value, b_attn_out, b_down, ln1_gain, ln1_bias, ln2_gain, ln2_bias, b_up)
    vector = jnp.concatenate(small)
    lanes = packed_w.shape[2] + unit_width
    vector = jnp.pad(vector, (0, lanes - vector.shape[0]))
    sent = jnp.concatenate((packed_w, up_w), axis=2)
    sent = jnp.concatenate((sent, jnp.broadcast_to(vector, (GROUP, 1, lanes))), axis=1)
    got = plane_exchange(sent)
    qkv_rows = column_gather(got[:, :, : 3 * head_width], plane)
    mat_qkv = qkv_rows[:, :, :wrow].reshape(width, 3 * head_width)
    vectors = qkv_rows[:, :, wrow].reshape(count, 3 * head_width)
    bounds = [0]
    for piece in small:
        bounds.append(bounds[-1] + piece.shape[0])
    (
        vec_query,
        vec_value,
        vec_out,
        vec_down,
        gain_one,
        shift_one,
        gain_two,
        shift_two,
        vec_up,
    ) = [
        vectors[:, bounds[at] : bounds[at + 1]].reshape(-1).astype(f32)
        for at in range(len(small))
    ]
    vec_up = lax.dynamic_index_in_dim(
        vec_up.reshape(planes, GROUP, frow), place, 1, keepdims=False
    ).reshape(-1)
    zero_vec = jnp.zeros((head_width,), f32)
    vec_qkv = jnp.concatenate(
        (
            lax.dynamic_slice_in_dim(vec_query, place * head_width, head_width),
            zero_vec,
            lax.dynamic_slice_in_dim(vec_value, place * head_width, head_width),
        )
    )

    ffn_rows = lax.all_gather(
        jnp.concatenate(
            (got[:, :wrow, 3 * head_width :].reshape(-1, unit_width), w_down.reshape(-1, unit_width))
        ),
        "dp",
        axis=0,
        axis_index_groups=column_groups(),
    )
    mat_up = ffn_rows[:, : GROUP * wrow].reshape(width, unit_width)
    mat_down = ffn_rows[:, GROUP * wrow :].reshape(unit_width, width)
    mat_out = lax.all_gather(w_attn_out, "dp", axis=0, tiled=True)

    gathered_dy = plane_gather([grad_out[m] for m in both])
    groups = [(m, half) for m in both for half in range(2)]

    normed1 = {}
    packed = []
    for m in both:
        parts = []
        for half in range(2):
            values = gathered_x[m][half].reshape(-1, width).astype(f32)
            unit, _ = layer_norm_parts(values)
            normed1[m, half] = (unit * gain_one + shift_one).astype(bf16)
            parts.append(
                (mm(normed1[m, half], mat_qkv, NN) + vec_qkv)
                .astype(bf16)
                .reshape(4, row_count, 3 * head_width)
            )
        packed.append(jnp.concatenate(parts))
    packed = jnp.stack(packed)

    blocks = place ^ jnp.arange(GROUP, dtype=jnp.int32)
    slots = []
    for m in both:
        table = [0] * GROUP
        for at, mask in enumerate((0, FIRST[m], SECOND[m], FIRST[m] ^ SECOND[m])):
            table[mask] = at
            table[mask ^ 1] = at + 4
        hit = blocks[:, None] == jnp.arange(GROUP, dtype=jnp.int32)[None, :]
        slots.append(
            jnp.sum(jnp.where(hit, jnp.asarray(table, jnp.int32)[None, :], 0), axis=1)
        )
    order = jnp.stack(slots).astype(jnp.int32)
    parents = lax.dynamic_index_in_dim(leaf_parent, plane, 1, keepdims=False)
    heads = 2 * place + jnp.arange(2, dtype=jnp.int32)
    slopes = jnp.exp2(-8.0 * (heads.astype(f32) + 1.0) / HEADS)
    context, logs = attention_forward(order, parents, slopes, packed)
    own_context = plane_exchange(context)
    own_context = own_context.transpose(1, 2, 0, 3).reshape(micro_count * row_count, width)

    resid = tokens.reshape(-1, width).astype(f32)
    middle = resid + mm(own_context, mat_out, NN) + vec_out
    unit2, scale2 = layer_norm_parts(middle)
    normed2 = (unit2 * gain_two + shift_two).astype(bf16)
    normed2 = normed2.reshape(micro_count, row_count, width)
    gathered_a2 = plane_gather([normed2[m] for m in both])

    down_even, down_odd, back_even, back_odd = [], [], [], []
    grad_up = grad_down = grad_vec_up = 0.0
    for m, half in groups:
        a2 = gathered_a2[m][half].reshape(-1, width)
        dy = gathered_dy[m][half].reshape(-1, width)
        upper = mm(a2, mat_up, NN) + vec_up
        active, pull = jax.vjp(gelu_tanh, upper)
        active = active.astype(bf16)
        y_part = mm(active, mat_down, NN).reshape(4, row_count, width)
        du = pull(mm(dy, mat_down, NT))[0].astype(bf16)
        da_part = mm(du, mat_up, NT).reshape(4, row_count, width)
        (down_odd if half else down_even).append(y_part)
        (back_odd if half else back_even).append(da_part)
        grad_down = grad_down + mm(active, dy, TN)
        grad_up = grad_up + mm(a2, du, TN)
        grad_vec_up = grad_vec_up + jnp.sum(du, axis=0, dtype=f32)
    grad_normed2 = plane_scatter(back_even, back_odd)
    ffn_out = plane_scatter(down_even, down_odd)
    output = (
        middle.reshape(tokens.shape) + jnp.stack(ffn_out) + vec_down
    ).astype(bf16)

    grad_y = grad_out.reshape(-1, width).astype(f32)
    grad_normed2 = jnp.stack(grad_normed2).reshape(-1, width)
    grad_gain_two = jnp.sum(grad_normed2 * unit2, axis=0)
    grad_shift_two = jnp.sum(grad_normed2, axis=0)
    grad_middle = grad_y + layer_norm_back(grad_normed2, unit2, scale2, gain_two)
    grad_attn = grad_middle.astype(bf16)
    grad_ctx = mm(grad_attn, mat_out, NT).astype(bf16)
    grad_ctx = grad_ctx.reshape(micro_count, row_count, GROUP, head_width).transpose(2, 0, 1, 3)
    plane_grad_ctx = plane_exchange(grad_ctx)
    grad_out_mat = mm(own_context, grad_attn, TN)
    grad_vec_out = jnp.sum(grad_attn, axis=0, dtype=f32)
    grad_vec_down = jnp.sum(grad_y, axis=0)

    grad_packed = attention_backward(
        order, parents, slopes, packed, context, plane_grad_ctx, logs
    )
    grad_qkv = grad_vec_qkv = 0.0
    first_even, first_odd = [], []
    grad_gain_one = grad_shift_one = 0.0
    for m, half in groups:
        dqkv = grad_packed[m, 4 * half : 4 * half + 4].reshape(-1, 3 * head_width)
        da1 = mm(dqkv, mat_qkv, NT)
        (first_odd if half else first_even).append(da1.reshape(4, row_count, width))
        grad_qkv = grad_qkv + mm(normed1[m, half], dqkv, TN)
        grad_vec_qkv = grad_vec_qkv + jnp.sum(dqkv, axis=0, dtype=f32)
    grad_normed1 = jnp.stack(plane_scatter(first_even, first_odd)).reshape(-1, width)
    unit1, scale1 = layer_norm_parts(resid)
    grad_gain_one = jnp.sum(grad_normed1 * unit1, axis=0)
    grad_shift_one = jnp.sum(grad_normed1, axis=0)
    grad_input = grad_middle + layer_norm_back(grad_normed1, unit1, scale1, gain_one)
    grad_input = grad_input.astype(bf16).reshape(tokens.shape)

    sum_down = column_scatter(grad_down.reshape(planes, frow, width), plane)
    sum_up = column_scatter(grad_up.reshape(planes, GROUP * wrow, unit_width), plane)
    sum_qkv = column_scatter(grad_qkv.reshape(planes, GROUP * wrow, 3 * head_width), plane)
    home = plane_exchange(
        jnp.concatenate((sum_qkv, sum_up), axis=1).reshape(GROUP, wrow, lanes)
    )
    home_up = home[:, :, 3 * head_width :].reshape(GROUP, wrow, planes, frow)
    home_up = home_up.transpose(1, 2, 0, 3).reshape(wrow, -1)
    home_qkv = [
        home[:, :, at * head_width : (at + 1) * head_width].transpose(1, 0, 2).reshape(wrow, width)
        for at in range(3)
    ]
    sum_out = lax.psum_scatter(
        grad_out_mat.astype(bf16), "dp", scatter_dimension=0, tiled=True
    ).astype(f32)

    def placed(piece):
        return lax.dynamic_update_slice_in_dim(
            jnp.zeros((width,), f32), piece, place * head_width, 0
        )

    up_terms = lax.dynamic_update_slice_in_dim(
        jnp.zeros((planes, GROUP, frow), f32),
        grad_vec_up.reshape(planes, 1, frow),
        place,
        1,
    )
    terms = jnp.concatenate(
        [
            piece.reshape(count, -1)
            for piece in (
                placed(grad_vec_qkv[:head_width]),
                placed(grad_vec_qkv[2 * head_width :]),
                grad_vec_out,
                grad_vec_down,
                grad_gain_one,
                grad_shift_one,
                grad_gain_two,
                grad_shift_two,
                up_terms,
            )
        ],
        axis=1,
    )
    sums = jnp.sum(lax.all_to_all(terms, "dp", 0, 0, tiled=True), axis=0)
    pieces = [sums[bounds[at] : bounds[at + 1]] for at in range(len(small))]
    return (
        output,
        grad_input,
        home_qkv[0],
        home_qkv[1],
        home_qkv[2],
        sum_out,
        home_up,
        sum_down,
        pieces[0],
        pieces[1],
        pieces[2],
        pieces[8],
        pieces[3],
        pieces[4],
        pieces[5],
        pieces[6],
        pieces[7],
    )


def solution(mesh):
    row = P("dp", None)
    vec = P("dp")
    tok = P(None, "dp", None)
    return jax.shard_map(
        on_device,
        mesh=mesh,
        in_specs=(
            tok, tok, row, row, row, vec, vec, row, vec, row, vec, row, vec, vec, vec, vec, vec, P(),
        ),
        out_specs=(
            tok, tok, row, row, row, row, row, row, vec, vec, vec, vec, vec, vec, vec, vec, vec,
        ),
        check_vma=False,
    )
```

time: 1950 us -> 496 us (0.25)
  waiting for transfers between devices: 1030 us -> 193 us
  blocking collectives: 236 us -> 0 us
  local copies, waits for them, and re-layouts: 266 us -> 46.3 us
  matrix products: 148 us -> 64.1 us
  other arithmetic: 115 us -> 61.6 us
  starting transfers between devices: 120 us -> 77.7 us
  Pallas kernels: 0 us -> 28.3 us
    reduce_scatter x6 -> x1, waiting for transfers between devices: 678 us -> 24.2 us  [on_device(): lax.psum_scatter(grad_out_mat.astype(bf16), 'dp', scatter_dimension=0, ti...]
    unnamed x2 -> x0, blocking collectives: 195 us -> none
    another operation x104 -> x2, local copies, waits for them, and re-layouts: 147 us -> 0.01 us
    ppermute x28 -> x54, waiting for transfers between devices: 273 us -> 141 us  [swap(): lax.ppermute(value, 'dp', [(source, source ^ mask) for source in range(co...]
    dot_general x50 -> x39, matrix products: 148 us -> 64.1 us  [mm(): lax.dot_general(left, right, (contract, ((), ())), preferred_element_type...]
    all_gather x6 -> x2, waiting for transfers between devices: 71.2 us -> 0.02 us  [the longest x1 0.02 us: on_device(): lax.all_gather(jnp.concatenate((got[:, :wrow, 3 * head_width:].reshape(-1...]
    reduce_sum x30 -> x24, other arithmetic: 81.1 us -> 15.4 us  [the longest x6 4.8 us: layer_norm_parts(): spread = jnp.mean(center * center, axis=-1, keepdims=True)]
    ppermute x28 -> x54, starting transfers between devices: 119 us -> 58.2 us  [swap(): lax.ppermute(value, 'dp', [(source, source ^ mask) for source in range(co...]
  transfers between devices with their start and end apart: 40 -> 62, of which waited for: 13 -> 27; matrix products, arithmetic and copies ran while one was open for 16% -> 31% of each run, Pallas kernels for 0% -> 6%
where the time goes in v1:
time: 496 us; the launch traced here: 487 us
  waiting for transfers between devices  193 us (39%)
  starting transfers between devices  77.7 us (16%)
  matrix products  64.1 us (13%)
  other arithmetic  61.6 us (12%)
  local copies, waits for them, and re-layouts  46.3 us (9%)
  Pallas kernels  28.3 us (6%)
  between operations  16.2 us (3%)
    ppermute x54, waiting for transfers between devices, swap(): lax.ppermute(value, 'dp', [(source, source ^ mask) for source in range(co...  141 us
    dot_general x39, matrix products, mm(): lax.dot_general(left, right, (contract, ((), ())), preferred_element_type...  64.1 us
    ppermute x54, starting transfers between devices, swap(): lax.ppermute(value, 'dp', [(source, source ^ mask) for source in range(co...  58.2 us
    reduce_scatter x1, waiting for transfers between devices, on_device(): lax.psum_scatter(grad_out_mat.astype(bf16), 'dp', scatter_dimension=0, ti...  24.2 us
    all_to_all x4, waiting for transfers between devices, plane_exchange(): lax.all_to_all(value, 'dp', 0, 0, tiled=True, axis_index_groups=plane_gro...  22 us
    pallas_call x1, Pallas kernels, attention_backward(): pl.pallas_call(backward_kernel, out_shape=jax.ShapeDtypeStruct(packed.sha...  17.1 us
    all_to_all x4, starting transfers between devices, plane_exchange(): lax.all_to_all(value, 'dp', 0, 0, tiled=True, axis_index_groups=plane_gro...  16.1 us
    unnamed x226, local copies, waits for them, and re-layouts  14.2 us
  transfers between devices with their start and end apart: 62, of which 27 were waited for; matrix products, arithmetic and copies ran while one was open for 31% of the time, Pallas kernels for 6%

profile of v1, /device:TPU:0, one launch (start us, length us, event | category | flops | bytes accessed | tf_op | source)
XLA Modules:
  0.0 487.1 jit_solution(12311834786664256178)
XLA Ops:
  9.9 5.2 %all-to-all-start = ((bf16[8,33,896]{2,1,0:T(8,128)(2,1)}), bf16[8,33,896]{2,1,0:T(8,128)(2,1)S(1)}, u32[]{:S(2)}, u32[]{:S(2)}) async-start(bf16[8,33,896]{2,1,0:T(8,128)(2,1)} %pad_maximum_fusion.26), calls=%async_computation | async-start | bytes 1146880 | tf_op jit(solution)/shard_map/all_to_all | solution.py:72
  15.3 10.1 %all-to-all-done = bf16[8,33,896]{2,1,0:T(8,128)(2,1)S(1)} async-done(((bf16[8,33,896]{2,1,0:T(8,128)(2,1)}), bf16[8,33,896]{2,1,0:T(8,128)(2,1)S(1)}, u32[]{:S(2)}, u32[]{:S(2)}) %all-to-all-start) | async-done | bytes 473120 | tf_op jit(solution)/shard_map/all_to_all | solution.py:72
  42.4 3.7 collective-permute-start.4
  52.0 4.5 collective-permute-done.4
  57.0 25.9 %collective-permute-done.3 = bf16[8,33,384]{2,0,1:T(8,128)(2,1)S(1)} collective-permute-done((bf16[8,33,384]{2,0,1:T(8,128)(2,1)S(1)}, bf16[8,33,384]{2,0,1:T(8,128)(2,1)S(1)}, u32[]{:S(2)}, u32[]{:S(2)}) %collective-permute-start.3) | collective-permute-done | bytes 202784 | tf_op jit(solution)/shard_map/ppermute | solution.py:37
  96.8 3.6 collective-permute-done.33
  100.4 5.9 %collective-permute-done.26 = bf16[2,160,1024]{2,1,0:T(8,128)(2,1)} collective-permute-done((bf16[2,160,1024]{2,1,0:T(8,128)(2,1)}, bf16[2,160,1024]{2,1,0:T(8,128)(2,1)}, u32[]{:S(2)}, u32[]{:S(2)}) %collective-permute-start.26) | collective-permute-done | bytes 655392 | tf_op jit(solution)/shard_map/ppermute | solution.py:37
  109.8 3.3 fusion.23
  117.7 11.2 %tree_attention.1 = (bf16[8,2,160,128]{3,2,1,0:T(8,128)(2,1)}, f32[2,8,1280]{2,1,0:T(8,128)S(1)}) custom-call(s32[2,8]{1,0:T(2,128)S(1)} %pad_add_fusion.order_ref, s32[2,8]{1,0:T(2,128)S(1)} %bitcast.363, f32[2]{0:T(128)S(1)} %multiply_exponential_fusion.slope_ref, bf16[2,8,160,384]{3,2,1,0:T(8,128)(2,1)S(1)} %pad_maximum_fusion.packed_ref), custom_call_target="tpu_custom_call" | custom-call | flops 4000000000 | bytes 3000000 | tf_op jit(solution)/shard_map/tree_attention/pallas_call | solution.py:424
  128.9 3.7 all-to-all-start.1
  142.4 4.0 all-to-all-done.1
  160.3 3.9 collective-permute-start.11
  165.8 4.5 collective-permute-start.19
  178.8 7.7 %collective-permute-done.19 = bf16[2,160,1024]{2,1,0:T(8,128)(2,1)} collective-permute-done((bf16[2,160,1024]{2,1,0:T(8,128)(2,1)}, bf16[2,160,1024]{2,1,0:T(8,128)(2,1)}, u32[]{:S(2)}, u32[]{:S(2)}) %collective-permute-start.19) | collective-permute-done | bytes 655392 | tf_op jit(solution)/shard_map/ppermute | solution.py:37
  190.6 4.3 collective-permute-done.12
  230.8 16.2 %collective-permute-done.49 = bf16[256,512]{1,0:T(8,128)(2,1)S(1)} collective-permute-done((bf16[256,512]{1,0:T(8,128)(2,1)S(1)}, bf16[256,512]{1,0:T(8,128)(2,1)S(1)}, u32[]{:S(2)}, u32[]{:S(2)}) %collective-permute-start.49) | collective-permute-done | bytes 262176 | tf_op jit(solution)/shard_map/ppermute | solution.py:37
  247.1 11.7 %collective-permute-start.51 = (bf16[128,1024]{1,0:T(8,128)(2,1)S(1)}, bf16[128,1024]{1,0:T(8,128)(2,1)}, u32[]{:S(2)}, u32[]{:S(2)}) collective-permute-start(bf16[128,1024]{1,0:T(8,128)(2,1)S(1)} %get-tuple-element.42), channel_id=1, source_target_pairs={{0,8},{1,9},{2,10},{3,11},{4,12},{5,13},{6,14},{7,15},{8,0},{9,1},... | collective-permute-start | bytes 786440 | tf_op jit(solution)/shard_map/ppermute | solution.py:37
  263.5 5.5 %collective-permute-done.51 = bf16[128,1024]{1,0:T(8,128)(2,1)} collective-permute-done((bf16[128,1024]{1,0:T(8,128)(2,1)S(1)}, bf16[128,1024]{1,0:T(8,128)(2,1)}, u32[]{:S(2)}, u32[]{:S(2)}) %collective-permute-start.51) | collective-permute-done | bytes 262176 | tf_op jit(solution)/shard_map/ppermute | solution.py:37
  283.4 7.7 %collective-permute-done.23 = bf16[2,160,1024]{2,1,0:T(8,128)(2,1)S(1)} collective-permute-done((bf16[2,160,1024]{2,1,0:T(8,128)(2,1)S(1)}, bf16[2,160,1024]{2,1,0:T(8,128)(2,1)S(1)}, u32[]{:S(2)}, u32[]{:S(2)}) %collective-permute-start.23) | collective-permute-done | bytes 655392 | tf_op jit(solution)/shard_map/ppermute | solution.py:37
  292.8 11.4 %collective-permute-done.37 = bf16[2,160,1024]{2,1,0:T(8,128)(2,1)S(1)} collective-permute-done((bf16[2,160,1024]{2,1,0:T(8,128)(2,1)S(1)}, bf16[2,160,1024]{2,1,0:T(8,128)(2,1)S(1)}, u32[]{:S(2)}, u32[]{:S(2)}) %collective-permute-start.37) | collective-permute-done | bytes 655392 | tf_op jit(solution)/shard_map/ppermute | solution.py:37
  305.2 3.3 collective-permute-done.30
  311.8 9.7 %collective-permute-done.38 = bf16[160,1024]{1,0:T(8,128)(2,1)S(1)} collective-permute-done((bf16[160,1024]{1,0:T(8,128)(2,1)S(1)}, bf16[160,1024]{1,0:T(8,128)(2,1)S(1)}, u32[]{:S(2)}, u32[]{:S(2)}) %collective-permute-start.38) | collective-permute-done | bytes 327712 | tf_op jit(solution)/shard_map/ppermute | solution.py:37
  325.5 4.0 convolution_convert_fusion
  333.5 3.5 all-to-all-start.2
  343.5 4.7 all-to-all-done.2.grad_ref
  349.7 17.1 %tree_attention_back.1 = bf16[2,8,160,384]{3,2,1,0:T(8,128)(2,1)S(1)} custom-call(s32[2,8]{1,0:T(2,128)S(1)} %pad_add_fusion.order_ref, s32[2,8]{1,0:T(2,128)S(1)} %bitcast.364, f32[2]{0:T(128)S(1)} %multiply_exponential_fusion.slope_ref, bf16[2,8,160,384]{3,2,1,0:T(8,128)(2,1)S(1)} %copy-done.3, bf16[8,2,160,128]{3,2,1,0:T(8,128)(2,1)} %get-tuple-element.19.ctx_ref, ...), custom_call_target="tpu_custom_call" | custom-call | flops 10000000000 | bytes 6000000 | tf_op jit(solution)/shard_map/tree_attention_back/pallas_call | solution.py:454
  389.3 9.3 %collective-permute-done.46 = bf16[256,384]{1,0:T(8,128)(2,1)} collective-permute-done((bf16[256,384]{1,0:T(8,128)(2,1)S(1)}, bf16[256,384]{1,0:T(8,128)(2,1)}, u32[]{:S(2)}, u32[]{:S(2)}) %collective-permute-start.46) | collective-permute-done | bytes 196640 | tf_op jit(solution)/shard_map/ppermute | solution.py:37
  404.6 3.7 all-to-all-start.3
  412.5 15.0 %collective-permute-done.40 = bf16[2,160,1024]{2,1,0:T(8,128)(2,1)} collective-permute-done((bf16[2,160,1024]{2,1,0:T(8,128)(2,1)}, bf16[2,160,1024]{2,1,0:T(8,128)(2,1)}, u32[]{:S(2)}, u32[]{:S(2)}) %collective-permute-start.40) | collective-permute-done | bytes 655392 | tf_op jit(solution)/shard_map/ppermute | solution.py:37
  429.7 3.2 all-to-all-done.3
  448.5 4.8 all-to-all-done.4
  454.4 24.2 %reduce-scatter.2.cloned.1.call-done = bf16[32,1024]{1,0:T(8,128)(2,1)} async-done(((bf16[1024,1024]{1,0:T(8,128)(2,1)}), bf16[32,1024]{1,0:T(8,128)(2,1)}) %reduce-scatter.2.cloned.1.call-update) | async-done | bytes 65552 | tf_op jit(solution)/shard_map/reduce_scatter | solution.py:689
  (528 shorter events, 214.4 us)
Async XLA Ops:
  15.1 131.8 %all-gather.6.cloned.1.call-start = ((), (), s32[]{:S(2)}) async-start(), calls=%async_computation.8 | async-start | bytes 2621440 | tf_op jit(solution)/shard_map/all_gather | solution.py:566
  27.0 124.2 %all-gather.4.cloned.1.call-start = ((), (), s32[]{:S(2)}) async-start(), calls=%async_computation.6 | async-start | bytes 2162688 | tf_op jit(solution)/shard_map/all_gather | solution.py:576
  39.9 48.7 %collective-permute-start.1 = (bf16[2,160,1024]{2,1,0:T(8,128)(2,1)}, bf16[2,160,1024]{2,1,0:T(8,128)(2,1)}, u32[]{:S(2)}, u32[]{:S(2)}) collective-permute-start(bf16[2,160,1024]{2,1,0:T(8,128)(2,1)} %pad_maximum_fusion.20), channel_id=1, source_target_pairs={{0,4},{1,5},{2,6},{3,7},{4,0},{5,1},{6,2},{7,3},{8,12},{9,13},{10,... | collective-permute-start | bytes 1966088 | tf_op jit(solution)/shard_map/ppermute | solution.py:37
  46.1 36.9 %collective-permute-start.3 = (bf16[8,33,384]{2,0,1:T(8,128)(2,1)S(1)}, bf16[8,33,384]{2,0,1:T(8,128)(2,1)S(1)}, u32[]{:S(2)}, u32[]{:S(2)}) collective-permute-start(bf16[8,33,384]{2,0,1:T(8,128)(2,1)S(1)} %copy.92), channel_id=1, source_target_pairs={{0,16},{1,17},{2,18},{3,19},{4,20},{5,21},{6,22},{7,23},{8,24},{9,... | collective-permute-start | bytes 608264 | tf_op jit(solution)/shard_map/ppermute | solution.py:37
  46.6 36.3 %collective-permute-start.2 = (bf16[8,33,384]{2,0,1:T(8,128)(2,1)S(1)}, bf16[8,33,384]{2,0,1:T(8,128)(2,1)S(1)}, u32[]{:S(2)}, u32[]{:S(2)}) collective-permute-start(bf16[8,33,384]{2,0,1:T(8,128)(2,1)S(1)} %copy.92), channel_id=1, source_target_pairs={{0,8},{1,9},{2,10},{3,11},{4,12},{5,13},{6,14},{7,15},{8,0},{9,1},... | collective-permute-start | bytes 608264 | tf_op jit(solution)/shard_map/ppermute | solution.py:37
  50.1 44.2 %collective-permute-start.5 = (bf16[2,160,1024]{2,1,0:T(8,128)(2,1)}, bf16[2,160,1024]{2,1,0:T(8,128)(2,1)}, u32[]{:S(2)}, u32[]{:S(2)}) collective-permute-start(bf16[2,160,1024]{2,1,0:T(8,128)(2,1)} %pad_maximum_fusion.20), channel_id=1, source_target_pairs={{0,1},{1,0},{2,3},{3,2},{4,5},{5,4},{6,7},{7,6},{8,9},{9,8},{10,11... | collective-permute-start | bytes 1966088 | tf_op jit(solution)/shard_map/ppermute | solution.py:37
  56.5 35.3 %collective-permute-start.8 = (bf16[2,160,1024]{2,1,0:T(8,128)(2,1)}, bf16[2,160,1024]{2,1,0:T(8,128)(2,1)S(1)}, u32[]{:S(2)}, u32[]{:S(2)}) collective-permute-start(bf16[2,160,1024]{2,1,0:T(8,128)(2,1)} %pad_maximum_fusion.21), channel_id=1, source_target_pairs={{0,2},{1,3},{2,0},{3,1},{4,6},{5,7},{6,4},{7,5},{8,10},{9,11},{10,... | collective-permute-start | bytes 1966088 | tf_op jit(solution)/shard_map/ppermute | solution.py:37
  94.8 42.6 %collective-permute-start.34 = (bf16[2,160,1024]{2,1,0:T(8,128)(2,1)}, bf16[2,160,1024]{2,1,0:T(8,128)(2,1)}, u32[]{:S(2)}, u32[]{:S(2)}) collective-permute-start(bf16[2,160,1024]{2,1,0:T(8,128)(2,1)} %pad_maximum_fusion.25), channel_id=1, source_target_pairs={{0,1},{1,0},{2,3},{3,2},{4,5},{5,4},{6,7},{7,6},{8,9},{9,8},{10,11... | collective-permute-start | bytes 1966088 | tf_op jit(solution)/shard_map/ppermute | solution.py:37
  96.3 43.6 %collective-permute-start.27 = (bf16[2,160,1024]{2,1,0:T(8,128)(2,1)}, bf16[2,160,1024]{2,1,0:T(8,128)(2,1)}, u32[]{:S(2)}, u32[]{:S(2)}) collective-permute-start(bf16[2,160,1024]{2,1,0:T(8,128)(2,1)} %pad_maximum_fusion.24), channel_id=1, source_target_pairs={{0,1},{1,0},{2,3},{3,2},{4,5},{5,4},{6,7},{7,6},{8,9},{9,8},{10,11... | collective-permute-start | bytes 1966088 | tf_op jit(solution)/shard_map/ppermute | solution.py:37
  100.4 37.0 %collective-permute-start.35 = (bf16[2,160,1024]{2,1,0:T(8,128)(2,1)}, bf16[2,160,1024]{2,1,0:T(8,128)(2,1)}, u32[]{:S(2)}, u32[]{:S(2)}) collective-permute-start(bf16[2,160,1024]{2,1,0:T(8,128)(2,1)} %collective-permute-done.33), channel_id=1, source_target_pairs={{0,1},{1,0},{2,3},{3,2},{4,5},{5,4},{6,7},{7,6},{8,9},{9,8},{10,11... | collective-permute-start | bytes 1966088 | tf_op jit(solution)/shard_map/ppermute | solution.py:37
  106.3 33.6 %collective-permute-start.28 = (bf16[2,160,1024]{2,1,0:T(8,128)(2,1)}, bf16[2,160,1024]{2,1,0:T(8,128)(2,1)}, u32[]{:S(2)}, u32[]{:S(2)}) collective-permute-start(bf16[2,160,1024]{2,1,0:T(8,128)(2,1)} %collective-permute-done.26), channel_id=1, source_target_pairs={{0,1},{1,0},{2,3},{3,2},{4,5},{5,4},{6,7},{7,6},{8,9},{9,8},{10,11... | collective-permute-start | bytes 1966088 | tf_op jit(solution)/shard_map/ppermute | solution.py:37
  165.8 20.7 %collective-permute-start.19 = (bf16[2,160,1024]{2,1,0:T(8,128)(2,1)}, bf16[2,160,1024]{2,1,0:T(8,128)(2,1)}, u32[]{:S(2)}, u32[]{:S(2)}) collective-permute-start(bf16[2,160,1024]{2,1,0:T(8,128)(2,1)} %pad_maximum_fusion.23), channel_id=1, source_target_pairs={{0,2},{1,3},{2,0},{3,1},{4,6},{5,7},{6,4},{7,5},{8,10},{9,11},{10,... | collective-permute-start | bytes 1966088 | tf_op jit(solution)/shard_map/ppermute | solution.py:37
  176.6 25.4 %collective-permute-start.20 = (bf16[2,160,1024]{2,1,0:T(8,128)(2,1)}, bf16[2,160,1024]{2,1,0:T(8,128)(2,1)S(1)}, u32[]{:S(2)}, u32[]{:S(2)}) collective-permute-start(bf16[2,160,1024]{2,1,0:T(8,128)(2,1)} %pad_maximum_fusion.23), channel_id=1, source_target_pairs={{0,1},{1,0},{2,3},{3,2},{4,5},{5,4},{6,7},{7,6},{8,9},{9,8},{10,11... | collective-permute-start | bytes 1966088 | tf_op jit(solution)/shard_map/ppermute | solution.py:37
  178.7 28.4 %collective-permute-start.13 = (bf16[2,160,1024]{2,1,0:T(8,128)(2,1)S(1)}, bf16[2,160,1024]{2,1,0:T(8,128)(2,1)S(1)}, u32[]{:S(2)}, u32[]{:S(2)}) collective-permute-start(bf16[2,160,1024]{2,1,0:T(8,128)(2,1)S(1)} %pad_maximum_fusion.22), channel_id=1, source_target_pairs={{0,1},{1,0},{2,3},{3,2},{4,5},{5,4},{6,7},{7,6},{8,9},{9,8},{10,11... | collective-permute-start | bytes 1966088 | tf_op jit(solution)/shard_map/ppermute | solution.py:37
  206.9 64.2 %collective-permute-start.22 = (bf16[4,160,1024]{2,1,0:T(8,128)(2,1)}, bf16[4,160,1024]{2,1,0:T(8,128)(2,1)}, u32[]{:S(2)}, u32[]{:S(2)}) collective-permute-start(bf16[4,160,1024]{2,1,0:T(8,128)(2,1)} %convolution_convert_fusion.5), channel_id=1, source_target_pairs={{0,1},{1,0},{2,3},{3,2},{4,5},{5,4},{6,7},{7,6},{8,9},{9,8},{10,11... | collective-permute-start | bytes 3932168 | tf_op jit(solution)/shard_map/ppermute | solution.py:37
  213.1 60.4 %collective-permute-start.15 = (bf16[4,160,1024]{2,1,0:T(8,128)(2,1)}, bf16[4,160,1024]{2,1,0:T(8,128)(2,1)}, u32[]{:S(2)}, u32[]{:S(2)}) collective-permute-start(bf16[4,160,1024]{2,1,0:T(8,128)(2,1)} %convolution_convert_fusion.6), channel_id=1, source_target_pairs={{0,1},{1,0},{2,3},{3,2},{4,5},{5,4},{6,7},{7,6},{8,9},{9,8},{10,11... | collective-permute-start | bytes 3932168 | tf_op jit(solution)/shard_map/ppermute | solution.py:37
  217.8 29.2 %collective-permute-start.49 = (bf16[256,512]{1,0:T(8,128)(2,1)S(1)}, bf16[256,512]{1,0:T(8,128)(2,1)S(1)}, u32[]{:S(2)}, u32[]{:S(2)}) collective-permute-start(bf16[256,512]{1,0:T(8,128)(2,1)S(1)} %get-tuple-element.47), channel_id=1, source_target_pairs={{0,16},{1,17},{2,18},{3,19},{4,20},{5,21},{6,22},{7,23},{8,24},{9,... | collective-permute-start | bytes 786440 | tf_op jit(solution)/shard_map/ppermute | solution.py:37
  217.8 29.2 %collective-permute-start.48 = (bf16[256,512]{1,0:T(8,128)(2,1)S(1)}, bf16[256,512]{1,0:T(8,128)(2,1)S(1)}, u32[]{:S(2)}, u32[]{:S(2)}) collective-permute-start(bf16[256,512]{1,0:T(8,128)(2,1)S(1)} %get-tuple-element.45), channel_id=1, source_target_pairs={{0,8},{1,9},{2,10},{3,11},{4,12},{5,13},{6,14},{7,15},{8,0},{9,1},... | collective-permute-start | bytes 786440 | tf_op jit(solution)/shard_map/ppermute | solution.py:37
  226.6 20.5 %collective-permute-start.53 = (bf16[128,1024]{1,0:T(8,128)(2,1)S(1)}, bf16[128,1024]{1,0:T(8,128)(2,1)S(1)}, u32[]{:S(2)}, u32[]{:S(2)}) collective-permute-start(bf16[128,1024]{1,0:T(8,128)(2,1)S(1)} %get-tuple-element.43), channel_id=1, source_target_pairs={{0,24},{1,25},{2,26},{3,27},{4,28},{5,29},{6,30},{7,31},{8,16},{9,... | collective-permute-start | bytes 786440 | tf_op jit(solution)/shard_map/ppermute | solution.py:37
  247.0 30.5 %collective-permute-start.36 = (bf16[4,160,1024]{2,1,0:T(8,128)(2,1)}, bf16[4,160,1024]{2,1,0:T(8,128)(2,1)}, u32[]{:S(2)}, u32[]{:S(2)}) collective-permute-start(bf16[4,160,1024]{2,1,0:T(8,128)(2,1)} %convolution_convert_fusion.3), channel_id=1, source_target_pairs={{0,1},{1,0},{2,3},{3,2},{4,5},{5,4},{6,7},{7,6},{8,9},{9,8},{10,11... | collective-permute-start | bytes 3932168 | tf_op jit(solution)/shard_map/ppermute | solution.py:37
  247.1 21.9 %collective-permute-start.51 = (bf16[128,1024]{1,0:T(8,128)(2,1)S(1)}, bf16[128,1024]{1,0:T(8,128)(2,1)}, u32[]{:S(2)}, u32[]{:S(2)}) collective-permute-start(bf16[128,1024]{1,0:T(8,128)(2,1)S(1)} %get-tuple-element.42), channel_id=1, source_target_pairs={{0,8},{1,9},{2,10},{3,11},{4,12},{5,13},{6,14},{7,15},{8,0},{9,1},... | collective-permute-start | bytes 786440 | tf_op jit(solution)/shard_map/ppermute | solution.py:37
  276.8 33.2 %collective-permute-start.16 = (bf16[2,160,1024]{2,1,0:T(8,128)(2,1)S(1)}, bf16[2,160,1024]{2,1,0:T(8,128)(2,1)S(1)}, u32[]{:S(2)}, u32[]{:S(2)}) collective-permute-start(bf16[2,160,1024]{2,1,0:T(8,128)(2,1)S(1)} %slice.436), channel_id=1, source_target_pairs={{0,4},{1,5},{2,6},{3,7},{4,0},{5,1},{6,2},{7,3},{8,12},{9,13},{10,... | collective-permute-start | bytes 1966088 | tf_op jit(solution)/shard_map/ppermute | solution.py:37
  280.2 24.0 %collective-permute-start.37 = (bf16[2,160,1024]{2,1,0:T(8,128)(2,1)S(1)}, bf16[2,160,1024]{2,1,0:T(8,128)(2,1)S(1)}, u32[]{:S(2)}, u32[]{:S(2)}) collective-permute-start(bf16[2,160,1024]{2,1,0:T(8,128)(2,1)S(1)} %slice.433), channel_id=1, source_target_pairs={{0,2},{1,3},{2,0},{3,1},{4,6},{5,7},{6,4},{7,5},{8,10},{9,11},{10,... | collective-permute-start | bytes 1966088 | tf_op jit(solution)/shard_map/ppermute | solution.py:37
  282.4 26.1 %collective-permute-start.30 = (bf16[2,160,1024]{2,1,0:T(8,128)(2,1)S(1)}, bf16[2,160,1024]{2,1,0:T(8,128)(2,1)S(1)}, u32[]{:S(2)}, u32[]{:S(2)}) collective-permute-start(bf16[2,160,1024]{2,1,0:T(8,128)(2,1)S(1)} %slice.434), channel_id=1, source_target_pairs={{0,4},{1,5},{2,6},{3,7},{4,0},{5,1},{6,2},{7,3},{8,12},{9,13},{10,... | collective-permute-start | bytes 1966088 | tf_op jit(solution)/shard_map/ppermute | solution.py:37
  292.1 45.7 %collective-permute-start.24 = (bf16[160,1024]{1,0:T(8,128)(2,1)}, bf16[160,1024]{1,0:T(8,128)(2,1)}, u32[]{:S(2)}, u32[]{:S(2)}) collective-permute-start(bf16[160,1024]{1,0:T(8,128)(2,1)} %fusion.105), channel_id=1, source_target_pairs={{0,4},{1,5},{2,6},{3,7},{4,0},{5,1},{6,2},{7,3},{8,12},{9,13},{10,... | collective-permute-start | bytes 983048 | tf_op jit(solution)/shard_map/ppermute | solution.py:37
  311.0 30.1 %collective-permute-start.17 = (bf16[160,1024]{1,0:T(8,128)(2,1)}, bf16[160,1024]{1,0:T(8,128)(2,1)}, u32[]{:S(2)}, u32[]{:S(2)}) collective-permute-start(bf16[160,1024]{1,0:T(8,128)(2,1)} %fusion.104), channel_id=1, source_target_pairs={{0,2},{1,3},{2,0},{3,1},{4,6},{5,7},{6,4},{7,5},{8,10},{9,11},{10,... | collective-permute-start | bytes 983048 | tf_op jit(solution)/shard_map/ppermute | solution.py:37
  337.1 141.5 %reduce-scatter.2.cloned.1.call-start = ((), (), s32[]{:S(2)}) async-start(), calls=%async_computation.7 | async-start | bytes 2162688 | tf_op jit(solution)/shard_map/reduce_scatter | solution.py:689
  371.3 28.7 %collective-permute-start.39 = (bf16[4,160,1024]{2,1,0:T(8,128)(2,1)}, bf16[4,160,1024]{2,1,0:T(8,128)(2,1)}, u32[]{:S(2)}, u32[]{:S(2)}) collective-permute-start(bf16[4,160,1024]{2,1,0:T(8,128)(2,1)} %convolution_convert_fusion.2), channel_id=1, source_target_pairs={{0,1},{1,0},{2,3},{3,2},{4,5},{5,4},{6,7},{7,6},{8,9},{9,8},{10,11... | collective-permute-start | bytes 3932168 | tf_op jit(solution)/shard_map/ppermute | solution.py:37
  388.3 20.0 %collective-permute-start.43 = (bf16[2,160,1024]{2,1,0:T(8,128)(2,1)}, bf16[2,160,1024]{2,1,0:T(8,128)(2,1)}, u32[]{:S(2)}, u32[]{:S(2)}) collective-permute-start(bf16[2,160,1024]{2,1,0:T(8,128)(2,1)} %slice.431), channel_id=1, source_target_pairs={{0,2},{1,3},{2,0},{3,1},{4,6},{5,7},{6,4},{7,5},{8,10},{9,11},{10,... | collective-permute-start | bytes 1966088 | tf_op jit(solution)/shard_map/ppermute | solution.py:37
  403.1 24.4 %collective-permute-start.40 = (bf16[2,160,1024]{2,1,0:T(8,128)(2,1)}, bf16[2,160,1024]{2,1,0:T(8,128)(2,1)}, u32[]{:S(2)}, u32[]{:S(2)}) collective-permute-start(bf16[2,160,1024]{2,1,0:T(8,128)(2,1)} %slice.432), channel_id=1, source_target_pairs={{0,4},{1,5},{2,6},{3,7},{4,0},{5,1},{6,2},{7,3},{8,12},{9,13},{10,... | collective-permute-start | bytes 1966088 | tf_op jit(solution)/shard_map/ppermute | solution.py:37
  404.6 28.3 %all-to-all-start.3 = ((f32[8,32,896]{2,1,0:T(8,128)}), f32[8,32,896]{2,1,0:T(8,128)S(1)}, u32[]{:S(2)}, u32[]{:S(2)}) async-start(f32[8,32,896]{2,1,0:T(8,128)} %bitcast.105), calls=%async_computation.3 | async-start | bytes 1835008 | tf_op jit(solution)/shard_map/all_to_all | solution.py:72
  410.6 27.9 %collective-permute-start.44 = (bf16[160,1024]{1,0:T(8,128)(2,1)}, bf16[160,1024]{1,0:T(8,128)(2,1)}, u32[]{:S(2)}, u32[]{:S(2)}) collective-permute-start(bf16[160,1024]{1,0:T(8,128)(2,1)} %fusion.109), channel_id=1, source_target_pairs={{0,4},{1,5},{2,6},{3,7},{4,0},{5,1},{6,2},{7,3},{8,12},{9,13},{10,... | collective-permute-start | bytes 983048 | tf_op jit(solution)/shard_map/ppermute | solution.py:37
  (138 other events, 945.5 us)
Sparse Core Ops, SparseCore 0:
  27.2 62.5 all-gather.5
  92.6 57.8 all-gather.3
  340.2 138.4 reduce-scatter.1
